TPU v7x, 32 devices: a whole 2x2x4 slice. The times are simulated.
32 devices in a mesh: dp: 16 (over z, y, core), ctx: 2 (over x).
Axes of the slice: x: 2, y: 2, z: 4, core: 2. Of those that a mesh axis runs over, the one named last changes fastest.
Arguments:
- tokens: bfloat16 [16384, 768], P(('dp', 'ctx')), may hold values from -6 to 6
- out_grad: bfloat16 [16384, 768], P(('dp', 'ctx')), may hold values from -6 to 6
- segments: int32 [16384], P(('dp', 'ctx')), may hold values from 0 to 3, as said below
- positions: int32 [16384], P(('dp', 'ctx')), may hold values from 0 to 717, as said below
- params: float32 [32, 221472], P(('dp', 'ctx')), may hold values from -3 to 3
- first_moment: float32 [32, 221472], P(('dp', 'ctx')), may hold values from -0.0009765625 to 0.0009765625
- second_moment: float32 [32, 221472], P(('dp', 'ctx')), may hold values from 3.6686354e-09 to 2.9631286e-08
Outputs:
- result: bfloat16 [16384, 768], P(('dp', 'ctx'))
- input_grad: float32 [16384, 768], P(('dp', 'ctx'))
- grads: float32 [32, 221472], P(('dp', 'ctx'))
- new_params: float32 [32, 221472], P(('dp', 'ctx'))
- new_first: float32 [32, 221472], P(('dp', 'ctx'))
- new_second: float32 [32, 221472], P(('dp', 'ctx'))
Inputs may be any that keep to these rules, and one draw needn't show every extreme that they name: `segments`: within each sequence of 1024 tokens the segment numbers start at 0, never fall, and count exactly 4 documents. `positions`: each token's position is its distance from the first token of its document.
All inputs are finite; a program needn't handle non-finite values.
Results may differ from a plain program's by a relative error of at most 0.0087.
The roundings to bfloat16 on the way count: a program that leaves them out, or rounds other values in their place, can miss the bound.
Values may be sent and summed in bfloat16 or wider, within the bound.
No kernel may reach another device: no remote copies, remote signals or barrier semaphores. Data moves between devices by JAX's collectives and lax.ppermute only.
A program may use at most 192 MiB of HBM per device.

v0:
```python
import jax
import jax.numpy as jnp
from jax import lax
from jax.sharding import PartitionSpec as P

D = 768
HEADS = 12
HEAD_DIM = 64
ROT = 16
FF = 3072


norm_eps = 1e-05
beta_first = 0.9
beta_second = 0.95
learn_rate = 0.01
weight_decay = 0.01
adam_eps = 1e-08
adam_steps = 3
rope_base = 10000.0


def from_behind(shard, axis, by):
    peers = lax.axis_size(axis)
    pairs = [(i, i + by) for i in range(peers) if 0 <= i + by < peers]
    return lax.ppermute(shard, axis, pairs)


def split_rows(row_block, owners):
    height_list = [D, D, D, FF]
    breadth_list = [3 * D, D, FF, D]
    number = row_block.shape[0]
    pieces = []
    offset = 0
    for height, breadth in zip(height_list, breadth_list):
        extent = height // owners * breadth
        pieces.append(
            row_block[:, offset : offset + extent].reshape(number * (height // owners), breadth)
        )
        offset += extent
    extent = (8 * D + FF) // owners
    pieces.append(row_block[:, offset : offset + extent].reshape(number * extent))
    return pieces


def pack_rows(pieces, owners):
    number = pieces[0].shape[0] // (D // owners)
    return jnp.concatenate([section.reshape(number, -1) for section in pieces], axis=1)


def split_vector(vector):
    lengths = [D, D, D, FF, D, D, D, D, D]
    pieces = []
    offset = 0
    for extent in lengths:
        pieces.append(vector[offset : offset + extent].astype(jnp.float32))
        offset += extent
    return pieces


def normalize(inputs):
    centred = inputs - jnp.mean(inputs, axis=1, keepdims=True)
    inverse = lax.rsqrt(jnp.mean(centred * centred, axis=1, keepdims=True) + norm_eps)
    return (centred * inverse, inverse)


def rotary_tables(positions):
    halfway = ROT // 2
    frequency = jnp.power(rope_base, -jnp.arange(halfway, dtype=jnp.float32) * (2.0 / ROT))
    angles = positions.astype(jnp.float32)[:, None] * frequency[None, :]
    cosine = jnp.cos(angles)
    sine_table = jnp.sin(angles)
    return (
        jnp.concatenate([cosine, cosine], axis=1)[:, None, :],
        jnp.concatenate([sine_table, sine_table], axis=1)[:, None, :],
    )


def rotate(tensor, cosine, sine_table):
    halfway = ROT // 2
    turned = tensor[..., :ROT]
    swapped = jnp.concatenate([-turned[..., halfway:], turned[..., :halfway]], axis=-1)
    return jnp.concatenate([turned * cosine + swapped * sine_table, tensor[..., ROT:]], axis=-1)


def rotate_back(tensor, cosine, sine_table):
    halfway = ROT // 2
    turned = tensor[..., :ROT]
    scaled = turned * sine_table
    swapped = jnp.concatenate([scaled[..., halfway:], -scaled[..., :halfway]], axis=-1)
    return jnp.concatenate([turned * cosine + swapped, tensor[..., ROT:]], axis=-1)


def gelu_exact(inputs):
    return 0.5 * inputs * (1.0 + lax.erf(inputs * 0.7071067811865476))


def gelu_slope(inputs):
    return (
        0.5 * (1.0 + lax.erf(inputs * 0.7071067811865476))
        + inputs * jnp.exp(-0.5 * inputs * inputs) * 0.3989422804014327
    )


def head_scores(query_rows, key_rows, allowed):
    scores = jnp.dot(query_rows, key_rows.T, preferred_element_type=jnp.float32) * HEAD_DIM ** (
        -0.5
    )
    return jnp.where(allowed, scores, -jnp.inf)


def head_forward(query_rows, key_rows, value_rows, allowed):
    scores = head_scores(query_rows, key_rows, allowed)
    highest = jnp.max(scores, axis=1, keepdims=True)
    logsum = highest + jnp.log(jnp.sum(jnp.exp(scores - highest), axis=1, keepdims=True))
    weights = jnp.exp(scores - logsum).astype(jnp.bfloat16)
    output = jnp.dot(weights, value_rows, preferred_element_type=jnp.float32).astype(jnp.bfloat16)
    return (output, logsum[:, 0])


def head_backward(query_rows, key_rows, value_rows, output, grad_output, logsum, allowed):
    scores = head_scores(query_rows, key_rows, allowed)
    probability = jnp.exp(scores - logsum[:, None])
    grad_probability = jnp.dot(grad_output, value_rows.T, preferred_element_type=jnp.float32)
    row_delta = jnp.sum(
        grad_output.astype(jnp.float32) * output.astype(jnp.float32), axis=1, keepdims=True
    )
    grad_scores = (probability * (grad_probability - row_delta) * HEAD_DIM ** (-0.5)).astype(
        jnp.bfloat16
    )
    grad_query = jnp.dot(grad_scores, key_rows, preferred_element_type=jnp.float32)
    grad_keys = jnp.dot(grad_scores.T, query_rows, preferred_element_type=jnp.float32)
    grad_values = jnp.dot(
        probability.astype(jnp.bfloat16).T, grad_output, preferred_element_type=jnp.float32
    )
    return (grad_query, grad_keys, grad_values)


def adam_update(params, grads, first_moment, second_moment, squares_total):
    clip_factor = jnp.minimum(1.0, 1.0 / jnp.sqrt(squares_total + 1e-12))
    clipped = grads * clip_factor
    new_first = beta_first * first_moment + (1.0 - beta_first) * clipped
    new_second = beta_second * second_moment + (1.0 - beta_second) * clipped * clipped
    corrected_first = new_first / (1.0 - beta_first**adam_steps)
    corrected_second = new_second / (1.0 - beta_second**adam_steps)
    new_params = params - learn_rate * (
        corrected_first / (jnp.sqrt(corrected_second) + adam_eps) + weight_decay * params
    )
    return (new_params, new_first, new_second)


def on_device(tokens, out_grad, segments, positions, params, first_moment, second_moment):
    owners = lax.axis_size("dp") * lax.axis_size("ctx")
    shards = split_rows(params.astype(jnp.bfloat16), owners)
    w_qkv, w_dense, w_up, w_down, vector = (
        lax.all_gather(shards[0], ("dp", "ctx"), axis=0, tiled=True),
        lax.all_gather(shards[1], ("dp", "ctx"), axis=0, tiled=True),
        lax.all_gather(shards[2], ("dp", "ctx"), axis=0, tiled=True),
        lax.all_gather(shards[3], ("dp", "ctx"), axis=0, tiled=True),
        lax.all_gather(shards[4], ("dp", "ctx"), axis=0, tiled=True),
    )
    bias_q, bias_v, bias_dense, bias_up, bias_down, gain_one, shift_one, gain_two, shift_two = (
        split_vector(vector)
    )
    rows_here = tokens.shape[0]
    half_index = lax.axis_index("ctx")
    inputs = tokens.astype(jnp.float32)
    normed, inverse = normalize(inputs)
    attn_in = (normed * gain_one + shift_one).astype(jnp.bfloat16)
    mlp_in = (normed * gain_two + shift_two).astype(jnp.bfloat16)
    projected = jnp.dot(attn_in, w_qkv, preferred_element_type=jnp.float32)
    cosine, sine_table = rotary_tables(positions)
    query_all = rotate(
        (projected[:, :D] + bias_q).reshape(rows_here, HEADS, HEAD_DIM), cosine, sine_table
    ).astype(jnp.bfloat16)
    key_all = rotate(
        projected[:, D : 2 * D].reshape(rows_here, HEADS, HEAD_DIM), cosine, sine_table
    ).astype(jnp.bfloat16)
    value_all = (
        (projected[:, 2 * D :] + bias_v).astype(jnp.bfloat16).reshape(rows_here, HEADS, HEAD_DIM)
    )
    query_heads = query_all.transpose(1, 0, 2)
    key_heads = key_all.transpose(1, 0, 2)
    value_heads = value_all.transpose(1, 0, 2)
    far_keys, far_values, far_segments = from_behind(
        (key_heads, value_heads, segments.astype(jnp.bfloat16)), "ctx", 1
    )
    keys_joined = jnp.concatenate([far_keys, key_heads], axis=1)
    values_joined = jnp.concatenate([far_values, value_heads], axis=1)
    segments_joined = jnp.concatenate([far_segments.astype(jnp.int32), segments])
    query_place = half_index * rows_here + jnp.arange(rows_here, dtype=jnp.int32)
    key_place = (half_index - 1) * rows_here + jnp.arange(2 * rows_here, dtype=jnp.int32)
    allowed = (
        (key_place[None, :] <= query_place[:, None])
        & (key_place[None, :] >= 0)
        & (segments_joined[None, :] == segments[:, None])
    )

    def forward_head(bundle):
        return head_forward(bundle[0], bundle[1], bundle[2], allowed)

    outputs, logsums = lax.map(forward_head, (query_heads, keys_joined, values_joined))
    attended = outputs.transpose(1, 0, 2).reshape(rows_here, D)
    attn_out = jnp.dot(attended, w_dense, preferred_element_type=jnp.float32) + bias_dense
    hidden_pre = jnp.dot(mlp_in, w_up, preferred_element_type=jnp.float32) + bias_up
    activated = gelu_exact(hidden_pre).astype(jnp.bfloat16)
    mlp_out = jnp.dot(activated, w_down, preferred_element_type=jnp.float32) + bias_down
    result = (inputs + attn_out + mlp_out).astype(jnp.bfloat16)
    w_qkv, w_dense, w_up, w_down = (
        lax.all_gather(shards[0], ("dp", "ctx"), axis=0, tiled=True),
        lax.all_gather(shards[1], ("dp", "ctx"), axis=0, tiled=True),
        lax.all_gather(shards[2], ("dp", "ctx"), axis=0, tiled=True),
        lax.all_gather(shards[3], ("dp", "ctx"), axis=0, tiled=True),
    )
    cotangent = out_grad.astype(jnp.float32)
    grad_down = jnp.dot(activated.T, out_grad, preferred_element_type=jnp.float32)
    grad_bias_out = jnp.sum(cotangent, axis=0)
    grad_hidden = jnp.dot(out_grad, w_down.T, preferred_element_type=jnp.float32) * gelu_slope(
        hidden_pre
    )
    grad_hidden_low = grad_hidden.astype(jnp.bfloat16)
    grad_up = jnp.dot(mlp_in.T, grad_hidden_low, preferred_element_type=jnp.float32)
    grad_bias_up = jnp.sum(grad_hidden, axis=0)
    grad_mlp_in = jnp.dot(grad_hidden_low, w_up.T, preferred_element_type=jnp.float32)
    grad_dense = jnp.dot(attended.T, out_grad, preferred_element_type=jnp.float32)
    grad_attended = jnp.dot(out_grad, w_dense.T, preferred_element_type=jnp.float32).astype(
        jnp.bfloat16
    )
    grad_att_heads = grad_attended.reshape(rows_here, HEADS, HEAD_DIM).transpose(1, 0, 2)

    def backward_head(bundle):
        return head_backward(
            bundle[0], bundle[1], bundle[2], bundle[3], bundle[4], bundle[5], allowed
        )

    grad_qh, grad_kh, grad_vh = lax.map(
        backward_head, (query_heads, keys_joined, values_joined, outputs, grad_att_heads, logsums)
    )
    back_keys, back_values = (
        from_behind(grad_kh[:, :rows_here].astype(jnp.bfloat16), "ctx", -1).astype(jnp.float32),
        from_behind(grad_vh[:, :rows_here].astype(jnp.bfloat16), "ctx", -1).astype(jnp.float32),
    )
    grad_kh_near = grad_kh[:, rows_here:] + back_keys
    grad_vh_near = grad_vh[:, rows_here:] + back_values
    grad_query = rotate_back(grad_qh.transpose(1, 0, 2), cosine, sine_table).reshape(rows_here, D)
    grad_key = rotate_back(grad_kh_near.transpose(1, 0, 2), cosine, sine_table).reshape(
        rows_here, D
    )
    grad_value = grad_vh_near.transpose(1, 0, 2).reshape(rows_here, D)
    grad_low = jnp.concatenate([grad_query, grad_key, grad_value], axis=1).astype(jnp.bfloat16)
    grad_qkv = jnp.dot(attn_in.T, grad_low, preferred_element_type=jnp.float32)
    grad_attn_in = jnp.dot(grad_low, w_qkv.T, preferred_element_type=jnp.float32)
    grad_normed = grad_attn_in * gain_one + grad_mlp_in * gain_two
    grad_inputs = cotangent + inverse * (
        grad_normed
        - jnp.mean(grad_normed, axis=1, keepdims=True)
        - normed * jnp.mean(grad_normed * normed, axis=1, keepdims=True)
    )
    grad_vector = jnp.concatenate(
        [
            jnp.sum(grad_query, axis=0),
            jnp.sum(grad_value, axis=0),
            grad_bias_out,
            grad_bias_up,
            grad_bias_out,
            jnp.sum(grad_attn_in * normed, axis=0),
            jnp.sum(grad_attn_in, axis=0),
            jnp.sum(grad_mlp_in * normed, axis=0),
            jnp.sum(grad_mlp_in, axis=0),
        ]
    )
    summed = (
        lax.psum_scatter(grad_qkv, ("dp", "ctx"), scatter_dimension=0, tiled=True),
        lax.psum_scatter(grad_dense, ("dp", "ctx"), scatter_dimension=0, tiled=True),
        lax.psum_scatter(grad_up, ("dp", "ctx"), scatter_dimension=0, tiled=True),
        lax.psum_scatter(grad_down, ("dp", "ctx"), scatter_dimension=0, tiled=True),
        lax.psum_scatter(grad_vector, ("dp", "ctx"), scatter_dimension=0, tiled=True),
    )
    grads = pack_rows(list(summed), owners)
    squares_total = lax.psum(jnp.sum(grads * grads), ("dp", "ctx"))
    new_params, new_first, new_second = adam_update(
        params, grads, first_moment, second_moment, squares_total
    )
    return (result, grad_inputs, grads, new_params, new_first, new_second)


def solution(mesh):
    placed = (
        P(("dp", "ctx"), None),
        P(("dp", "ctx"), None),
        P(("dp", "ctx")),
        P(("dp", "ctx")),
        P(("dp", "ctx"), None),
        P(("dp", "ctx"), None),
        P(("dp", "ctx"), None),
    )
    return jax.shard_map(
        on_device,
        mesh=mesh,
        in_specs=placed,
        out_specs=(
            P(("dp", "ctx"), None),
            P(("dp", "ctx"), None),
            P(("dp", "ctx"), None),
            P(("dp", "ctx"), None),
            P(("dp", "ctx"), None),
            P(("dp", "ctx"), None),
        ),
        check_vma=False,
    )
```

profile of v0, /device:TPU:0, one launch (start us, length us, event | category | flops | bytes accessed | tf_op | source)
XLA Modules:
  0.0 845.9 jit_solution(10046025779379378541)
XLA Ops:
  13.9 4.9 collective-permute-start.1
  20.0 39.9 %all-reduce = bf16[9216]{0:T(1024)(128)(2,1)S(1)} all-reduce(bf16[9216]{0:T(1024)(128)(2,1)S(1)} %dynamic-update-slice), channel_id=2, replica_groups=mesh['dp'=16,'ctx'=2] {'dp','ctx'}, use_global_device_ids=true, to_apply=%add | all-reduce | flops 9216 | bytes 36864
  60.7 13.6 %all-gather.6.cloned.1.call-done = bf16[768,2304]{1,0:T(8,128)(2,1)} async-done(((bf16[24,2304]{1,0:T(8,128)(2,1)}), bf16[768,2304]{1,0:T(8,128)(2,1)}) %all-gather.6.cloned.1.call-update) | async-done | bytes 3538960 | tf_op jit(solution)/shard_map/all_gather | solution.py:156
  74.3 4.1 fusion.90
  80.0 3.0 copy.38
  89.6 4.2 collective-permute-start
  94.9 2.3 collective-permute-start.2
  97.4 34.3 %all-gather.8.cloned.1.call-done = bf16[768,768]{1,0:T(8,128)(2,1)} async-done(((bf16[24,768]{1,0:T(8,128)(2,1)}), bf16[768,768]{1,0:T(8,128)(2,1)}) %all-gather.8.cloned.1.call-update) | async-done | bytes 1179664 | tf_op jit(solution)/shard_map/all_gather | solution.py:157
  131.7 2.3 convolution_convert_fusion.1
  138.5 2.8 copy.42
  142.6 2.8 copy.43
  145.3 55.7 %while.28 = (s32[]{:T(128)}, bf16[12,512,64]{1,2,0:T(8,128)(2,1)}, f32[12,512]{1,0:T(8,128)S(1)}, bf16[12,512,64]{2,1,0:T(8,128)(2,1)}, bf16[12,1024,64]{2,1,0:T...) while((s32[]{:T(128)}, bf16[12,512,64]{1,2,0:T(8,128)(2,1)}, ...), condition=%wide.region_5.6_spmd.clone, body=%wide.region_2.5_spmd.clone.sunk | while | flops 140017152 | bytes 7046273 | solution.py:202
  201.1 3.3 fusion.101
  204.5 127.4 %while.29 = (s32[]{:T(128)}, f32[12,512,64]{1,2,0:T(8,128)}, f32[12,1024,64]{1,2,0:T(8,128)}, f32[12,1024,64]{1,2,0:T(8,128)}, bf16[12,512,64]{2,1,0:T(8,128)(2,...) while((s32[]{:T(128)}, f32[12,512,64]{1,2,0:T(8,128)}, ...), condition=%wide.region_8.9_spmd.clone, body=%wide.region_6.8_spmd.clone.sunk | while | flops 341966336 | bytes 11956381 | solution.py:236
  339.3 16.8 %collective-permute-done.3 = bf16[12,512,64]{1,2,0:T(8,128)(2,1)S(1)} collective-permute-done((bf16[12,512,64]{1,2,0:T(8,128)(2,1)S(1)}, bf16[12,512,64]{1,2,0:T(8,128)(2,1)S(1)}, u32[]{:S(2)}, u32[]{:S(2)}) %collective-permute-start.3) | collective-permute-done | bytes 786464 | tf_op jit(solution)/shard_map/ppermute | solution.py:26
  359.0 14.0 %collective-permute-done.4 = bf16[12,512,64]{1,2,0:T(8,128)(2,1)S(1)} collective-permute-done((bf16[12,512,64]{1,2,0:T(8,128)(2,1)S(1)}, bf16[12,512,64]{1,2,0:T(8,128)(2,1)S(1)}, u32[]{:S(2)}, u32[]{:S(2)}) %collective-permute-start.4) | collective-permute-done | bytes 786464 | tf_op jit(solution)/shard_map/ppermute | solution.py:26
  374.2 5.2 fusion.68
  379.7 8.2 multiply_convert_fusion.1
  387.9 7.5 fusion.99
  397.2 5.5 fusion.62
  402.7 8.5 %fusion.102 = f32[3072,768]{1,0:T(8,128)} fusion(bf16[512,3072]{1,0:T(8,128)(2,1)} %get-tuple-element.343, bf16[512,768]{1,0:T(8,128)(2,1)} %param.12), kind=kOutput, calls=%fused_computation.194 | convolution fusion | flops 2415919104 | bytes 13369344 | tf_op jit(solution)/shard_map/dot_general | solution.py:216
  413.4 6.3 fusion.64
  419.8 2.9 fusion.92
  424.5 41.0 %all-reduce.1 = f32[9216]{0:T(1024)S(1)} all-reduce(f32[9216]{0:T(1024)S(1)} %constant_dynamic-update-slice_fusion.6), channel_id=7, replica_groups=mesh['dp'=16,'ctx'=2] {'dp','ctx'}, use_global_device_ids=true, to_apply=%region_23.24.clone | all-reduce | flops 9216 | bytes 73728
  465.6 7.0 fusion.100
  473.6 26.2 %reduce-scatter.5.cloned.1.call-done = f32[24,2304]{1,0:T(8,128)} async-done(((f32[768,2304]{1,0:T(8,128)}), f32[24,2304]{1,0:T(8,128)}) %reduce-scatter.5.cloned.1.call-update) | async-done | bytes 221200 | tf_op jit(solution)/shard_map/reduce_scatter | solution.py:273
  501.0 139.8 %reduce-scatter.9.cloned.1.call-done = f32[24,3072]{1,0:T(8,128)} async-done(((f32[768,3072]{1,0:T(8,128)}), f32[24,3072]{1,0:T(8,128)}) %reduce-scatter.9.cloned.1.call-update) | async-done | bytes 294928 | tf_op jit(solution)/shard_map/reduce_scatter | solution.py:275
  642.1 139.7 %reduce-scatter.11.cloned.1.call-done = f32[96,768]{1,0:T(8,128)} async-done(((f32[3072,768]{1,0:T(8,128)}), f32[96,768]{1,0:T(8,128)}) %reduce-scatter.11.cloned.1.call-update) | async-done | bytes 294928 | tf_op jit(solution)/shard_map/reduce_scatter | solution.py:276
  783.2 2.5 multiply_reduce_fusion
  785.7 3.9 fusion.60
  789.6 39.8 %psum.7 = f32[]{:T(128)} all-reduce(f32[]{:T(128)} %multiply_reduce_fusion), channel_id=1, replica_groups=mesh['dp'=16,'ctx'=2] {'dp','ctx'}, use_global_device_ids=true, to_apply=%region_25.26 | all-reduce | flops 1 | bytes 8 | tf_op jit(solution)/shard_map/psum | solution.py:280
  830.1 8.5 %multiply_subtract_fusion = (f32[1,221472]{1,0:T(1,128)}, f32[1,221472]{1,0:T(1,128)}, f32[1,221472]{1,0:T(1,128)}) fusion(f32[1,221472]{1,0:T(1,128)S(1)} %copy-done.4, f32[1,221472]{1,0:T(1,128)S(1)} %constant_dynamic-update-slice_fusion.1, f32[]{:T(128)S(6)} %min.3, f32[1,221472]{1,0:T(1,128)S(1)} %copy-done.10, f32[1,221472]{1,0:T(1,128)} %param.17), kind=kLoop, calls=%fused_computation.109 | loop fusion | flops 3543552 | bytes 6201220 | tf_op jit(solution)/shard_map/sub | solution.py:146
  (329 shorter events, 228.3 us)
Async XLA Ops:
  7.2 6.7 copy-start.17
  7.2 52.8 %copy-start = (bf16[512,768]{1,0:T(8,128)(2,1)S(1)}, bf16[512,768]{1,0:T(8,128)(2,1)}, u32[]{:S(2)}) copy-start(bf16[512,768]{1,0:T(8,128)(2,1)} %param.11) | copy-start | bytes 2359300
  7.2 67.2 %all-gather.6.cloned.1.call-start = ((), (), s32[]{:S(2)}) async-start(), calls=%async_computation.4 | async-start | bytes 3649536 | tf_op jit(solution)/shard_map/all_gather | solution.py:156
  9.6 50.9 %copy-start.18 = (s32[512]{0:T(512)S(1)}, s32[512]{0:T(512)}, u32[]{:S(2)}) copy-start(s32[512]{0:T(512)} %param.14) | copy-start | bytes 6148
  10.4 121.2 %all-gather.8.cloned.1.call-start = ((), (), s32[]{:S(2)}) async-start(), calls=%async_computation.5 | async-start | bytes 1216512 | tf_op jit(solution)/shard_map/all_gather | solution.py:157
  11.4 368.3 %all-gather.10.cloned.1.call-start = ((), (), s32[]{:S(2)}) async-start(), calls=%async_computation.6 | async-start | bytes 4866048 | tf_op jit(solution)/shard_map/all_gather | solution.py:158
  13.9 374.0 %all-gather.12.cloned.1.call-start = ((), (), s32[]{:S(2)}) async-start(), calls=%async_computation.7 | async-start | bytes 4866048 | tf_op jit(solution)/shard_map/all_gather | solution.py:159
  13.9 83.4 %collective-permute-start.1 = (bf16[512]{0:T(512)(128)(2,1)S(1)}, bf16[512]{0:T(512)(128)(2,1)S(1)}, u32[]{:S(2)}, u32[]{:S(2)}) collective-permute-start(bf16[512]{0:T(512)(128)(2,1)S(1)} %convert_element_type.105), channel_id=1, source_target_pairs={{0,1},{2,3},{4,5},{6,7},{8,9},{10,11},{12,13},{14,15},{16,17},{18,... | collective-permute-start | bytes 3080 | tf_op jit(solution)/shard_map/ppermute | solution.py:26
  19.6 453.0 %reduce-scatter.7.cloned.1.call-start = ((), (), s32[]{:S(2)}) async-start(), calls=%async_computation.9 | async-start | bytes 2433024 | tf_op jit(solution)/shard_map/reduce_scatter | solution.py:274
  84.6 2.8 copy-start.1
  89.6 47.3 %collective-permute-start = (bf16[12,512,64]{1,2,0:T(8,128)(2,1)}, bf16[12,512,64]{1,2,0:T(8,128)(2,1)}, u32[]{:S(2)}, u32[]{:S(2)}) collective-permute-start(bf16[12,512,64]{1,2,0:T(8,128)(2,1)} %maximum_bitcast_fusion.1), channel_id=1, source_target_pairs={{0,1},{2,3},{4,5},{6,7},{8,9},{10,11},{12,13},{14,15},{16,17},{18,... | collective-permute-start | bytes 2359304 | tf_op jit(solution)/shard_map/ppermute | solution.py:26
  94.9 46.3 %collective-permute-start.2 = (bf16[12,512,64]{1,2,0:T(8,128)(2,1)}, bf16[12,512,64]{1,2,0:T(8,128)(2,1)}, u32[]{:S(2)}, u32[]{:S(2)}) collective-permute-start(bf16[12,512,64]{1,2,0:T(8,128)(2,1)} %bitcast.159), channel_id=1, source_target_pairs={{0,1},{2,3},{4,5},{6,7},{8,9},{10,11},{12,13},{14,15},{16,17},{18,... | collective-permute-start | bytes 2359304 | tf_op jit(solution)/shard_map/ppermute | solution.py:26
  138.4 2.8 copy-start.5
  145.3 55.7 %copy-start.7 = (bf16[512,768]{1,0:T(8,128)(2,1)S(1)}, bf16[512,768]{1,0:T(8,128)(2,1)}, u32[]{:S(2)}) copy-start(bf16[512,768]{1,0:T(8,128)(2,1)} %param.12) | copy-start | bytes 2359300
  204.4 295.4 %reduce-scatter.5.cloned.1.call-start = ((), (), s32[]{:S(2)}) async-start(), calls=%async_computation.8 | async-start | bytes 7299072 | tf_op jit(solution)/shard_map/reduce_scatter | solution.py:273
  333.4 22.7 %copy-start.9 = (f32[12,1024,64]{1,2,0:T(8,128)S(1)}, f32[12,1024,64]{1,2,0:T(8,128)}, u32[]{:S(2)}) copy-start(f32[12,1024,64]{1,2,0:T(8,128)} %get-tuple-element.106) | copy-start | bytes 9437188
  333.4 22.6 %collective-permute-start.3 = (bf16[12,512,64]{1,2,0:T(8,128)(2,1)S(1)}, bf16[12,512,64]{1,2,0:T(8,128)(2,1)S(1)}, u32[]{:S(2)}, u32[]{:S(2)}) collective-permute-start(bf16[12,512,64]{1,2,0:T(8,128)(2,1)S(1)} %slice.265), channel_id=1, source_target_pairs={{1,0},{3,2},{5,4},{7,6},{9,8},{11,10},{13,12},{15,14},{17,16},{19,... | collective-permute-start | bytes 2359304 | tf_op jit(solution)/shard_map/ppermute | solution.py:26
  336.6 36.4 %collective-permute-start.4 = (bf16[12,512,64]{1,2,0:T(8,128)(2,1)S(1)}, bf16[12,512,64]{1,2,0:T(8,128)(2,1)S(1)}, u32[]{:S(2)}, u32[]{:S(2)}) collective-permute-start(bf16[12,512,64]{1,2,0:T(8,128)(2,1)S(1)} %slice.264), channel_id=1, source_target_pairs={{1,0},{3,2},{5,4},{7,6},{9,8},{11,10},{13,12},{15,14},{17,16},{19,... | collective-permute-start | bytes 2359304 | tf_op jit(solution)/shard_map/ppermute | solution.py:26
  358.7 14.2 %copy-start.2 = (f32[12,1024,64]{1,2,0:T(8,128)S(1)}, f32[12,1024,64]{1,2,0:T(8,128)}, u32[]{:S(2)}) copy-start(f32[12,1024,64]{1,2,0:T(8,128)} %get-tuple-element.107) | copy-start | bytes 9437188
  358.9 14.5 %copy-start.13 = (bf16[512,12,64]{0,2,1:T(8,128)(2,1)}, bf16[512,12,64]{0,2,1:T(8,128)(2,1)S(1)}, u32[]{:S(2)}) copy-start(bf16[512,12,64]{0,2,1:T(8,128)(2,1)S(1)} %fusion.67) | copy-start | bytes 2359300
  358.9 14.4 %copy-start.11 = (bf16[512,12,64]{0,2,1:T(8,128)(2,1)}, bf16[512,12,64]{0,2,1:T(8,128)(2,1)S(1)}, u32[]{:S(2)}) copy-start(bf16[512,12,64]{0,2,1:T(8,128)(2,1)S(1)} %pad_maximum_fusion.6) | copy-start | bytes 2359300
  379.4 261.4 %reduce-scatter.9.cloned.1.call-start = ((), (), s32[]{:S(2)}) async-start(), calls=%async_computation.10 | async-start | bytes 9732096 | tf_op jit(solution)/shard_map/reduce_scatter | solution.py:275
  395.4 1.7 copy-start.6
  402.7 379.1 %reduce-scatter.11.cloned.1.call-start = ((), (), s32[]{:S(2)}) async-start(), calls=%async_computation.11 | async-start | bytes 9732096 | tf_op jit(solution)/shard_map/reduce_scatter | solution.py:276
  413.3 6.4 copy-start.12
  413.3 6.4 copy-start.14
  413.4 6.4 copy-start.16
  413.4 6.4 copy-start.19
  419.8 2.9 copy-start.8
  783.2 46.9 %copy-start.3 = (f32[1,221472]{1,0:T(1,128)}, f32[1,221472]{1,0:T(1,128)S(1)}, u32[]{:S(2)}) copy-start(f32[1,221472]{1,0:T(1,128)S(1)} %constant_dynamic-update-slice_fusion.1) | copy-start | bytes 2657668
  785.7 44.4 %copy-start.4 = (f32[1,221472]{1,0:T(1,128)S(1)}, f32[1,221472]{1,0:T(1,128)}, u32[]{:S(2)}) copy-start(f32[1,221472]{1,0:T(1,128)} %param.15) | copy-start | bytes 2657668
  785.7 44.5 %copy-start.10 = (f32[1,221472]{1,0:T(1,128)S(1)}, f32[1,221472]{1,0:T(1,128)}, u32[]{:S(2)}) copy-start(f32[1,221472]{1,0:T(1,128)} %param.16) | copy-start | bytes 2657668
  (1 other events, 0.9 us)
Sparse Core Ops, SparseCore 0:
  11.5 62.8 all-gather.5
  77.8 53.7 all-gather.7
  135.2 63.8 all-gather.9
  201.9 61.9 all-gather.11
  269.0 97.9 reduce-scatter.6
  379.6 120.1 reduce-scatter.4
  505.7 135.0 reduce-scatter.8
  646.7 135.0 reduce-scatter.10
where the time goes:
time: 857 us; the launch traced here: 846 us
  waiting for transfers between devices  385 us (45%)
  matrix products  225 us (26%)
  blocking collectives  121 us (14%)
  local copies, waits for them, and re-layouts  47.7 us (6%)
  other arithmetic  36.3 us (4%)
  between operations  16 us (2%)
  starting transfers between devices  14.8 us (2%)
    reduce_scatter x1, waiting for transfers between devices, on_device(): lax.psum_scatter(grad_up, ('dp', 'ctx'), scatter_dimension=0, tiled=True)  140 us
    reduce_scatter x1, waiting for transfers between devices, on_device(): lax.psum_scatter(grad_down, ('dp', 'ctx'), scatter_dimension=0, tiled=True)  140 us
    unnamed x2, blocking collectives  80.8 us
    dot_general x24, matrix products, head_scores(): jnp.dot(query_rows, key_rows.T, preferred_element_type=jnp.float32)  46.7 us
    psum x1, blocking collectives, on_device(): squares_total = lax.psum(jnp.sum(grads * grads), ('dp', 'ctx'))  39.8 us
    all_gather x1, waiting for transfers between devices, on_device(): lax.all_gather(shards[1], ('dp', 'ctx'), axis=0, tiled=True)  34.3 us
    ppermute x5, waiting for transfers between devices, from_behind(): return lax.ppermute(shard, axis, pairs)  30.8 us
    reduce_scatter x1, waiting for transfers between devices, on_device(): lax.psum_scatter(grad_qkv, ('dp', 'ctx'), scatter_dimension=0, tiled=True)  26.2 us
  transfers between devices with their start and end apart: 13, of which 7 were waited for; matrix products, arithmetic and copies ran while one was open for 34% of the time, Pallas kernels for 0%

commit v1 on v0

v1 whole, which is shorter than its diff:
```python
import functools

import jax
import jax.numpy as jnp
from jax import lax
from jax.experimental import pallas as pl
from jax.experimental.pallas import tpu as pltpu
from jax.sharding import PartitionSpec as P

D = 768
HEADS = 12
HEAD_DIM = 64
ROT = 16
FF = 3072
HALF = D // 2
FFH = FF // 2
NVEC = 8 * D + FF
AX = ("dp", "ctx")
BF = jnp.bfloat16
F32 = jnp.float32

norm_eps = 1e-05
beta_first = 0.9
beta_second = 0.95
learn_rate = 0.01
weight_decay = 0.01
adam_eps = 1e-08
adam_steps = 3
rope_base = 10000.0
NEG = -1e30


def swap(value, mask):
    size = lax.axis_size("dp") * lax.axis_size("ctx")
    return lax.ppermute(value, AX, [(i, i ^ mask) for i in range(size)])


def pick(value, index, axis):
    return lax.dynamic_index_in_dim(value, index, axis, keepdims=False)


def gather_pair(both, rows_a):
    z_all = jnp.stack([both, swap(both, 8), swap(both, 16), swap(both, 24)])
    part_a, part_b = z_all[:, :rows_a], z_all[:, rows_a:]
    eight_a = jnp.stack([part_a, swap(part_a, 1)])
    eight_b = jnp.stack([part_b, swap(part_b, 4)])
    return eight_a, swap(eight_a, 4), eight_b, swap(eight_b, 1)


def rel_places(me, rel_z, rel_y, rel_x):
    outer = lax.shift_right_logical(me, 2)
    return outer ^ (rel_z * 2 + rel_y), (me & 1) ^ rel_x


def copy_all(copies):
    for one in copies:
        one.start()
    for one in copies:
        one.wait()


def assemble_pair_kernel(me_ref, a8, ay, b8, bx, out, sems):
    me = me_ref[0]
    copies = []
    for j in range(16):
        rel_z, rel_y, rel_x = j >> 2, (j >> 1) & 1, j & 1
        outer, xx = rel_places(me, rel_z, rel_y, rel_x)
        src_a = (ay if rel_y else a8).at[rel_x, rel_z]
        src_b = (bx if rel_x else b8).at[rel_y, rel_z]
        copies.append(pltpu.make_async_copy(src_a, out.at[outer, 0, xx], sems.at[2 * j]))
        copies.append(pltpu.make_async_copy(src_b, out.at[outer, 1, xx], sems.at[2 * j + 1]))
    copy_all(copies)


def assemble_down_kernel(me_ref, a8, ay, b8, bx, down, dense, sems):
    me = me_ref[0]
    copies = []
    for j in range(16):
        rel_z, rel_y, rel_x = j >> 2, (j >> 1) & 1, j & 1
        outer, xx = rel_places(me, rel_z, rel_y, rel_x)
        src_a = (ay if rel_y else a8).at[rel_x, rel_z]
        src_b = (bx if rel_x else b8).at[rel_y, rel_z]
        copies.append(pltpu.make_async_copy(src_a, down.at[outer, xx, pl.ds(0, 64)], sems.at[j]))
        copies.append(
            pltpu.make_async_copy(
                src_b.at[pl.ds(0, 32)], down.at[outer, xx, pl.ds(64, 32)], sems.at[16 + j]
            )
        )
        copies.append(
            pltpu.make_async_copy(src_b.at[pl.ds(32, 24)], dense.at[outer, xx], sems.at[32 + j])
        )
    copy_all(copies)


def whole(shape):
    return pl.BlockSpec(shape, lambda *_: (0,) * len(shape))


def assemble(kernel, me, pieces, shapes, sem_count):
    return pl.pallas_call(
        kernel,
        out_shape=[jax.ShapeDtypeStruct(s, BF) for s in shapes],
        in_specs=[pl.BlockSpec(memory_space=pltpu.SMEM)]
        + [pl.BlockSpec(memory_space=pl.ANY)] * 4,
        out_specs=[pl.BlockSpec(memory_space=pltpu.VMEM) for _ in shapes],
        scratch_shapes=[pltpu.SemaphoreType.DMA((sem_count,))],
        cost_estimate=pl.CostEstimate(flops=0, bytes_accessed=5_000_000, transcendentals=0),
    )(me.reshape(1), *pieces)


def rope_chunk(u, cosine, low, high):
    return u * cosine + pltpu.roll(u, 120, 1) * low + pltpu.roll(u, 8, 1) * high


def norm_rows(x_ref):
    inputs = x_ref[...].astype(F32)
    centred = inputs - jnp.mean(inputs, axis=1, keepdims=True)
    inverse = lax.rsqrt(jnp.mean(centred * centred, axis=1, keepdims=True) + norm_eps)
    return centred * inverse, inverse


def qkv_kernel(x_ref, w_ref, vec_ref, bias_ref, c_ref, lo_ref, hi_ref, q_ref, k_ref, v_ref, a1_ref, a2_ref):
    normed, _ = norm_rows(x_ref)
    a1 = (normed * vec_ref[0:1, :] + vec_ref[1:2, :]).astype(BF)
    a1_ref[...] = a1
    a2_ref[...] = (normed * vec_ref[2:3, :] + vec_ref[3:4, :]).astype(BF)
    proj = jnp.dot(a1, w_ref[:, : 3 * HALF], preferred_element_type=F32)
    cosine, low, high = c_ref[...], lo_ref[...], hi_ref[...]
    for j in range(3):
        at = slice(128 * j, 128 * j + 128)
        q = proj[:, 128 * j : 128 * j + 128] + bias_ref[0:1, at]
        q_ref[:, at] = (rope_chunk(q, cosine, low, high).astype(BF).astype(F32) * 0.125).astype(BF)
        k = proj[:, HALF + 128 * j : HALF + 128 * j + 128]
        k_ref[:, at] = rope_chunk(k, cosine, low, high).astype(BF)
    v_ref[...] = (proj[:, 2 * HALF :] + bias_ref[1:2, :]).astype(BF)


def far_kernel(used_ref, x_ref, w_ref, vec_ref, bias_ref, c_ref, lo_ref, hi_ref, k_ref, v_ref, a1_ref):
    @pl.when(used_ref[0] > 0)
    def _():
        normed, _ = norm_rows(x_ref)
        a1 = (normed * vec_ref[0:1, :] + vec_ref[1:2, :]).astype(BF)
        a1_ref[...] = a1
        proj = jnp.dot(a1, w_ref[:, HALF : 3 * HALF], preferred_element_type=F32)
        cosine, low, high = c_ref[...], lo_ref[...], hi_ref[...]
        for j in range(3):
            at = slice(128 * j, 128 * j + 128)
            k = proj[:, 128 * j : 128 * j + 128]
            k_ref[:, at] = rope_chunk(k, cosine, low, high).astype(BF)
        v_ref[...] = (proj[:, HALF:] + bias_ref[1:2, :]).astype(BF)

    @pl.when(used_ref[0] == 0)
    def _():
        k_ref[...] = jnp.zeros_like(k_ref)
        v_ref[...] = jnp.zeros_like(v_ref)
        a1_ref[...] = jnp.zeros_like(a1_ref)


def run_qkv(x, w, vecs, biases, tables, used=None):
    rows = x.shape[0]
    blk = 256
    row = lambda cols: pl.BlockSpec((blk, cols), lambda i, *_: (i, 0))
    specs = [row(D), whole(w.shape), whole(vecs.shape), whole(biases.shape)] + [row(128)] * 3
    wide = lambda cols: jax.ShapeDtypeStruct((rows, cols), BF)
    cost = pl.CostEstimate(flops=2 * rows * D * 3 * HALF, bytes_accessed=8_000_000, transcendentals=0)
    if used is None:
        return pl.pallas_call(
            qkv_kernel,
            grid=(rows // blk,),
            in_specs=specs,
            out_specs=[row(HALF)] * 3 + [row(D)] * 2,
            out_shape=[wide(HALF)] * 3 + [wide(D)] * 2,
            cost_estimate=cost,
        )(x, w, vecs, biases, *tables)
    return pl.pallas_call(
        far_kernel,
        grid_spec=pltpu.PrefetchScalarGridSpec(
            num_scalar_prefetch=1,
            grid=(rows // blk,),
            in_specs=specs,
            out_specs=[row(HALF)] * 2 + [row(D)],
        ),
        out_shape=[wide(HALF)] * 2 + [wide(D)],
        cost_estimate=cost,
    )(used, x, w, vecs, biases, *tables)


QB = 256


def variants(rows):
    cases = []
    for qb in range(rows // QB):
        for near in range(qb + 1):
            if near == 0:
                cases += [(qb, 0, far) for far in range(rows // QB + 1)]
            else:
                cases.append((qb, near, 0))
    return cases


def load_keys(far_ref, near_ref, rows, qb, near, far):
    parts = []
    if far:
        parts.append(far_ref[rows - far * QB : rows, :])
    parts.append(near_ref[near * QB : (qb + 1) * QB, :])
    return parts[0] if len(parts) == 1 else jnp.concatenate(parts, axis=0)


def attn_fwd_kernel(rows, plan_ref, q_ref, k_ref, v_ref, kf_ref, vf_ref, start_ref, o_ref, lse_ref):
    seq = pl.program_id(0)
    lane = lax.broadcasted_iota(jnp.int32, (QB, 128), 1)
    blocks = rows // QB
    for qb, near, far in variants(rows):
        low = plan_ref[seq * blocks + qb]
        match = low == (near if far == 0 else -far)

        @pl.when(match)
        def _(qb=qb, near=near, far=far):
            keys = load_keys(kf_ref, k_ref, rows, qb, near, far)
            values = load_keys(vf_ref, v_ref, rows, qb, near, far)
            count = keys.shape[0]
            first = near * QB - far * QB
            q = q_ref[qb * QB : (qb + 1) * QB, :]
            start = start_ref[qb * QB : (qb + 1) * QB, :]
            key_at = lax.broadcasted_iota(jnp.int32, (QB, count), 1) + first
            query_at = lax.broadcasted_iota(jnp.int32, (QB, count), 0) + qb * QB
            ok = (key_at >= start) & (key_at <= query_at)
            outs, lses = [], []
            for head in range(2):
                mine = (lane < 64) if head == 0 else (lane >= 64)
                qh = jnp.where(mine, q, jnp.zeros_like(q))
                s = lax.dot_general(qh, keys, (((1,), (1,)), ((), ())), preferred_element_type=F32)
                s = jnp.where(ok, s, NEG)
                top = jnp.max(s, axis=1, keepdims=True)
                e = jnp.exp(s - top)
                total = jnp.sum(e, axis=1, keepdims=True)
                prob = (e * (1.0 / total)).astype(BF)
                outs.append(jnp.dot(prob, values, preferred_element_type=F32))
                lses.append(jnp.broadcast_to(top + jnp.log(total), (QB, 128)))
            o_ref[qb * QB : (qb + 1) * QB, :] = jnp.where(lane < 64, outs[0], outs[1]).astype(BF)
            lse_ref[qb * QB : (qb + 1) * QB, :] = jnp.where(lane < 64, lses[0], lses[1])


def attn_bwd_kernel(
    rows, plan_ref, q_ref, k_ref, v_ref, kf_ref, vf_ref, start_ref, o_ref, do_ref, lse_ref,
    c_ref, lo_ref, hi_ref, cf_ref, lof_ref, hif_ref,
    dq_ref, dk_ref, dv_ref, dkf_ref, dvf_ref, sum_ref, dk_acc, dv_acc, lse_t, delta_t, start_t,
):
    seq = pl.program_id(0)
    blocks = rows // QB
    lane = lax.broadcasted_iota(jnp.int32, (QB, 128), 1)
    sub = lax.broadcasted_iota(jnp.int32, (128, QB), 0)
    dk_acc[...] = jnp.zeros_like(dk_acc)
    dv_acc[...] = jnp.zeros_like(dv_acc)
    lse_t[...] = jnp.transpose(lse_ref[...])
    delta_t[...] = jnp.transpose(do_ref[...].astype(F32) * o_ref[...].astype(F32))
    start_t[...] = jnp.transpose(jnp.broadcast_to(start_ref[...], (rows, 128)).astype(F32))[0:8, :]
    for qb, near, far in variants(rows):
        low = plan_ref[seq * blocks + qb]
        match = low == (near if far == 0 else -far)

        @pl.when(match)
        def _(qb=qb, near=near, far=far):
            keys = load_keys(kf_ref, k_ref, rows, qb, near, far)
            values = load_keys(vf_ref, v_ref, rows, qb, near, far)
            count = keys.shape[0]
            first = near * QB - far * QB
            at = slice(qb * QB, (qb + 1) * QB)
            q, do = q_ref[at, :], do_ref[at, :]
            start = start_t[0:1, at]
            key_at = lax.broadcasted_iota(jnp.int32, (count, QB), 0) + first
            query_at = lax.broadcasted_iota(jnp.int32, (count, QB), 1) + qb * QB
            ok = (key_at >= start.astype(jnp.int32)) & (key_at <= query_at)
            keys_t = jnp.transpose(keys)
            dqs, dk, dv = [], None, None
            for head in range(2):
                mine = (lane < 64) if head == 0 else (lane >= 64)
                hs = slice(64 * head, 64 * head + 64)
                qh = jnp.where(mine, q, jnp.zeros_like(q))
                doh = jnp.where(mine, do, jnp.zeros_like(do))
                lse = lse_t[64 * head : 64 * head + 1, at]
                delta = jnp.sum(delta_t[hs, at], axis=0, keepdims=True)
                nt = (((1,), (1,)), ((), ()))
                s = lax.dot_general(keys, qh, nt, preferred_element_type=F32)
                prob = jnp.where(ok, jnp.exp(s - lse), 0.0)
                dprob = lax.dot_general(values, doh, nt, preferred_element_type=F32)
                ds = (prob * (dprob - delta)).astype(BF)
                dv_h = jnp.dot(prob.astype(BF), doh, preferred_element_type=F32)
                dk_h = jnp.dot(ds, qh, preferred_element_type=F32)
                dv = dv_h if dv is None else dv + dv_h
                dk = dk_h if dk is None else dk + dk_h
                dqs.append(jnp.dot(keys_t, ds, preferred_element_type=F32))
            dq = jnp.transpose(jnp.where(sub < 64, dqs[0], dqs[1])) * 0.125
            dq = rope_chunk(dq, c_ref[at, :], -lo_ref[at, :], -hi_ref[at, :])
            dq_ref[at, :] = dq.astype(BF)
            part = jnp.sum(dq, axis=0, keepdims=True)
            if qb == 0:
                sum_ref[0:1, :] = part
            else:
                sum_ref[0:1, :] += part
            span = slice(rows + first, rows + first + count)
            dk_acc[span, :] += dk
            dv_acc[span, :] += dv
    dk_ref[...] = rope_chunk(dk_acc[rows:, :], c_ref[...], -lo_ref[...], -hi_ref[...]).astype(BF)
    dkf_ref[...] = rope_chunk(dk_acc[:rows, :], cf_ref[...], -lof_ref[...], -hif_ref[...]).astype(BF)
    dv_ref[...] = dv_acc[rows:, :].astype(BF)
    dvf_ref[...] = dv_acc[:rows, :].astype(BF)
    sum_ref[1:2, :] = jnp.sum(dv_acc[...], axis=0, keepdims=True)
    sum_ref[2:8, :] = jnp.zeros((6, 128), F32)


def attn_specs(rows):
    block = pl.BlockSpec((rows, 128), lambda s, p, *_: (s, p))
    per_seq = lambda cols: pl.BlockSpec((rows, cols), lambda s, p, *_: (s, 0))
    return block, per_seq


def attn_fwd(plan, q, k, v, kf, vf, start):
    total = q.shape[0]
    rows = total // 2
    block, per_seq = attn_specs(rows)
    return pl.pallas_call(
        functools.partial(attn_fwd_kernel, rows),
        grid_spec=pltpu.PrefetchScalarGridSpec(
            num_scalar_prefetch=1,
            grid=(2, HALF // 128),
            in_specs=[block] * 5 + [per_seq(1)],
            out_specs=[block] * 2,
        ),
        out_shape=[
            jax.ShapeDtypeStruct((total, HALF), BF),
            jax.ShapeDtypeStruct((total, HALF), F32),
        ],
        cost_estimate=pl.CostEstimate(
            flops=20_000_000_000, bytes_accessed=6_000_000, transcendentals=0
        ),
    )(plan, q, k, v, kf, vf, start)


def attn_bwd(plan, q, k, v, kf, vf, start, o, do, lse, tables, tables_far):
    total = q.shape[0]
    rows = total // 2
    block, per_seq = attn_specs(rows)
    wide = jax.ShapeDtypeStruct((total, HALF), BF)
    return pl.pallas_call(
        functools.partial(attn_bwd_kernel, rows),
        grid_spec=pltpu.PrefetchScalarGridSpec(
            num_scalar_prefetch=1,
            grid=(2, HALF // 128),
            in_specs=[block] * 5 + [per_seq(1)] + [block] * 3 + [per_seq(128)] * 6,
            out_specs=[block] * 5 + [pl.BlockSpec((8, 128), lambda s, p, *_: (s, p))],
            scratch_shapes=[pltpu.VMEM((2 * rows, 128), F32)] * 2
            + [pltpu.VMEM((128, rows), F32)] * 2
            + [pltpu.VMEM((8, rows), F32)],
        ),
        out_shape=[wide] * 5 + [jax.ShapeDtypeStruct((16, HALF), F32)],
        cost_estimate=pl.CostEstimate(
            flops=40_000_000_000, bytes_accessed=10_000_000, transcendentals=0
        ),
    )(plan, q, k, v, kf, vf, start, o, do, lse, *tables, *tables_far)


def rotary_tables(positions):
    halfway = ROT // 2
    frequency = jnp.power(rope_base, -jnp.arange(halfway, dtype=F32) * (2.0 / ROT))
    lane = jnp.arange(128) % HEAD_DIM
    angles = positions.astype(F32)[:, None] * frequency[lane % halfway][None, :]
    sine = jnp.sin(angles)
    cosine = jnp.where(lane < ROT, jnp.cos(angles), 1.0)
    low = jnp.where(lane < halfway, -sine, 0.0)
    high = jnp.where((lane >= halfway) & (lane < ROT), sine, 0.0)
    return cosine, low, high


def gelu_exact(inputs):
    return 0.5 * inputs * (1.0 + lax.erf(inputs * 0.7071067811865476))


def gelu_slope(inputs):
    return (
        0.5 * (1.0 + lax.erf(inputs * 0.7071067811865476))
        + inputs * jnp.exp(-0.5 * inputs * inputs) * 0.3989422804014327
    )


def normalize(inputs):
    centred = inputs - jnp.mean(inputs, axis=1, keepdims=True)
    inverse = lax.rsqrt(jnp.mean(centred * centred, axis=1, keepdims=True) + norm_eps)
    return (centred * inverse, inverse)


def adam_update(params, grads, first_moment, second_moment, squares_total):
    clip_factor = jnp.minimum(1.0, 1.0 / jnp.sqrt(squares_total + 1e-12))
    clipped = grads * clip_factor
    new_first = beta_first * first_moment + (1.0 - beta_first) * clipped
    new_second = beta_second * second_moment + (1.0 - beta_second) * clipped * clipped
    corrected_first = new_first / (1.0 - beta_first**adam_steps)
    corrected_second = new_second / (1.0 - beta_second**adam_steps)
    new_params = params - learn_rate * (
        corrected_first / (jnp.sqrt(corrected_second) + adam_eps) + weight_decay * params
    )
    return (new_params, new_first, new_second)


def split_shard(flat, owners):
    pieces, offset = [], 0
    for height, breadth in ((D, 3 * D), (D, D), (D, FF), (FF, D)):
        extent = height // owners * breadth
        pieces.append(flat[offset : offset + extent].reshape(height // owners, breadth))
        offset += extent
    pieces.append(flat[offset:])
    return pieces


def core_parts(qkv, dense):
    parts = []
    for c in range(2):
        cols = [qkv[:, D * j + HALF * c : D * j + HALF * c + HALF] for j in range(3)]
        parts.append((jnp.concatenate(cols, axis=1), dense[:, HALF * c : HALF * c + HALF]))
    return parts


def up_halves(up, group):
    rows = up.shape[0]
    four = up.reshape(rows, FF // (2 * group), 2, group)
    return four[:, :, 0].reshape(rows, FFH), four[:, :, 1].reshape(rows, FFH)


def gather_staged(me, core, qkv, dense, up, down, vector):
    group = 2 * down.shape[0]
    rows = qkv.shape[0]
    ups = up_halves(up, group)
    halves = core_parts(qkv, dense)
    lanes = jnp.pad(vector, (0, 384 - vector.shape[0])).reshape(3, 128)
    lanes = jnp.pad(lanes, ((0, rows - 3), (0, 0)))
    packed = [
        jnp.concatenate([halves[c][0], lanes, ups[c], halves[c][1]], axis=1) for c in range(2)
    ]
    is_zero = core == 0
    mine = jnp.where(is_zero, packed[0], packed[1])
    other = swap(jnp.where(is_zero, packed[1], packed[0]), 2)
    pair = jnp.where(is_zero, jnp.stack([mine, other]), jnp.stack([other, mine]))
    q_end, u_end = 3 * HALF + 128, 3 * HALF + 128 + FFH
    q_pieces = gather_pair(pair[:, :, :q_end], 1)
    u_pieces = gather_pair(pair[:, :, q_end:u_end], 1)
    dense_rows = jnp.concatenate([pair[0, :, u_end:], pair[1, :, u_end:]], axis=1)
    d_pieces = gather_pair(jnp.concatenate([down, dense_rows], axis=0), 64)
    return q_pieces, u_pieces, d_pieces


def finish_vector(w_q):
    lanes = w_q[:, :, :, :3, 3 * HALF :].reshape(32, 384)
    return lanes[:, : NVEC // 32].reshape(NVEC)


def split_vector(vector):
    pieces, offset = [], 0
    for extent in [D, D, D, FF, D, D, D, D, D]:
        pieces.append(vector[offset : offset + extent].astype(F32))
        offset += extent
    return pieces


def scatter_pair(part_a, part_b, place):
    z, y, x = place
    send_a = pick(part_a, 1 - x, 2).astype(BF)
    send_b = pick(part_b, 1 - y, 2).astype(BF)
    got_a, got_b = swap(send_a, 1), swap(send_b, 4)
    sum_a = pick(part_a, x, 2) + got_a.astype(F32)
    sum_b = pick(part_b, y, 2) + got_b.astype(F32)
    got_a = swap(pick(sum_a, 1 - y, 1).astype(BF), 4)
    got_b = swap(pick(sum_b, 1 - x, 1).astype(BF), 1)
    sum_a = pick(sum_a, y, 1) + got_a.astype(F32)
    sum_b = pick(sum_b, x, 1) + got_b.astype(F32)
    both = jnp.concatenate([sum_a, sum_b], axis=1)
    total = pick(both, z, 0)
    for k in (1, 2, 3):
        total = total + swap(pick(both, z ^ k, 0).astype(BF), 8 * k).astype(F32)
    return total


def on_device(tokens, out_grad, segments, positions, params, first_moment, second_moment):
    owners = lax.axis_size("dp") * lax.axis_size("ctx")
    staged = owners == 32
    me = (lax.axis_index("dp") * lax.axis_size("ctx") + lax.axis_index("ctx")).astype(jnp.int32)
    ctx, core = me & 1, (me >> 1) & 1
    is_zero = core == 0
    rows = tokens.shape[0]
    flat = params.reshape(-1)
    qkv, dense, up, down, vector = split_shard(flat.astype(BF), owners)
    group = 2 * down.shape[0]

    far_own = lax.ppermute(tokens, AX, [(i, i + 1) for i in range(0, owners, 2)])
    tokens_other = swap(tokens, 2)
    grad_other = swap(out_grad, 2)
    positions_all = jnp.concatenate([positions, swap(positions, 2)])

    if staged:
        q_pieces, u_pieces, d_pieces = gather_staged(me, core, qkv, dense, up, down, vector)
        w_q5 = assemble(assemble_pair_kernel, me, [p.reshape(p.shape[:2] + p.shape[-2:]) for p in q_pieces],
                        [(8, 2, 2, D // 32, 3 * HALF + 128)], 32)[0]
        w_u5 = assemble(assemble_pair_kernel, me, [p.reshape(p.shape[:2] + p.shape[-2:]) for p in u_pieces],
                        [(8, 2, 2, D // 32, FFH)], 32)[0]
        w_d4, dense5 = assemble(assemble_down_kernel, me, d_pieces,
                                [(8, 2, FF // 32, D), (8, 2, D // 32, D)], 48)
        vector = finish_vector(w_q5)
        w_q = w_q5.reshape(D, 3 * HALF + 128)
        w_up = w_u5.reshape(D, FFH)
        w_down = w_d4.reshape(FFH, D)
        dense_mine = dense5.reshape(8, 2, D // 32, 2, HALF).transpose(0, 3, 1, 2, 4).reshape(D, HALF)
        dense_got = swap(dense_mine, 2)
        w_dense = jnp.where(
            is_zero,
            jnp.concatenate([dense_mine, dense_got], axis=1),
            jnp.concatenate([dense_got, dense_mine], axis=1),
        )
    else:
        full = [lax.all_gather(p, AX, axis=0, tiled=True) for p in (qkv, dense, up, down, vector)]
        w_q = pick(full[0].reshape(D, 3, 2, HALF), core, 2).reshape(D, 3 * HALF)
        w_dense = full[1]
        w_up = pick(full[2].reshape(D, FFH // group, 2, group), core, 2).reshape(D, FFH)
        w_down = pick(full[3].reshape(FFH // group, 2, group, D), core, 1).reshape(FFH, D)
        vector = full[4]
    bias_q, bias_v, bias_dense, bias_up, bias_down, gain_one, shift_one, gain_two, shift_two = (
        split_vector(vector)
    )
    half_of = lambda v: jnp.where(is_zero, v[:HALF], v[HALF:])
    bias_up_half = pick(bias_up.reshape(FFH // group, 2, group), core, 1).reshape(FFH)
    dense_rows = lax.dynamic_slice_in_dim(w_dense, core * HALF, HALF, 0)
    vecs = jnp.stack([gain_one, shift_one, gain_two, shift_two] + [jnp.zeros_like(gain_one)] * 4)
    biases = jnp.stack([half_of(bias_q), half_of(bias_v)] + [jnp.zeros((HALF,), F32)] * 6)

    x_all = jnp.concatenate([tokens, tokens_other], axis=0)
    g_all = jnp.concatenate([out_grad, grad_other], axis=0)
    x_far = jnp.concatenate([far_own, swap(far_own, 2)], axis=0)
    local = jnp.arange(rows, dtype=jnp.int32)
    start = (jnp.concatenate([local, local]) - positions_all)[:, None]
    heads_pos = positions_all.reshape(2, rows)[:, :1]
    far_positions = jnp.maximum(heads_pos - rows + local[None, :], 0).reshape(-1)
    tables = rotary_tables(positions_all)
    tables_far = rotary_tables(far_positions)
    least = jnp.min(start.reshape(-1, QB), axis=1)
    blocks = rows // QB
    plan = jnp.where(least < 0, -((QB - 1 - least) // QB), least // QB)
    used = ctx.reshape(1)

    q, k, v, a1, a2 = run_qkv(x_all, w_q, vecs, biases, tables)
    kf, vf, a1f = run_qkv(x_far, w_q, vecs, biases, tables_far, used)
    att, lse = attn_fwd(plan, q, k, v, kf, vf, start)

    pre = jnp.dot(a2, w_up, preferred_element_type=F32) + bias_up_half
    act = gelu_exact(pre).astype(BF)
    grad_down = jnp.dot(act.T, g_all, preferred_element_type=F32)
    grad_dense = jnp.dot(att.T, g_all, preferred_element_type=F32)
    grad_pre = jnp.dot(g_all, w_down.T, preferred_element_type=F32) * gelu_slope(pre)
    grad_pre_low = grad_pre.astype(BF)
    grad_bias_up = jnp.sum(grad_pre, axis=0)
    grad_up = jnp.dot(a2.T, grad_pre_low, preferred_element_type=F32)

    grad_att = jnp.dot(g_all, dense_rows.T, preferred_element_type=F32).astype(BF)
    gq, gk, gv, gkf, gvf, sums = attn_bwd(
        plan, q, k, v, kf, vf, start, att, grad_att, lse, tables, tables_far
    )
    gkv = jnp.concatenate([gk, gv], axis=1)
    gkvf = jnp.concatenate([gkf, gvf], axis=1)
    grad_q_cols = jnp.dot(a1.T, gq, preferred_element_type=F32)
    grad_kv_cols = jnp.dot(a1.T, gkv, preferred_element_type=F32) + jnp.dot(
        a1f.T, gkvf, preferred_element_type=F32
    )
    grad_qkv = jnp.concatenate([grad_q_cols, grad_kv_cols], axis=1)

    normed, inverse = normalize(x_all.astype(F32))
    normed_far, _ = normalize(x_far.astype(F32))
    w_qkv = w_q[:, : 3 * HALF]
    ga1 = jnp.dot(gq, w_qkv[:, :HALF].T, preferred_element_type=F32) + jnp.dot(
        gkv, w_qkv[:, HALF:].T, preferred_element_type=F32
    )
    ga1f = jnp.dot(gkvf, w_qkv[:, HALF:].T, preferred_element_type=F32)
    ga2 = jnp.dot(grad_pre_low, w_up.T, preferred_element_type=F32)
    grad_gain_one = jnp.sum(ga1 * normed, axis=0) + jnp.sum(ga1f * normed_far, axis=0)
    grad_shift_one = jnp.sum(ga1, axis=0) + jnp.sum(ga1f, axis=0)
    grad_gain_two = jnp.sum(ga2 * normed, axis=0)
    grad_shift_two = jnp.sum(ga2, axis=0)

    cotangent = out_grad.astype(F32)
    grad_bias_out = jnp.sum(cotangent, axis=0)
    sums = jnp.sum(sums.reshape(2, 8, HALF), axis=0)
    nothing = jnp.zeros((HALF,), F32)
    spread = lambda v: jnp.where(
        is_zero, jnp.concatenate([v, nothing]), jnp.concatenate([nothing, v])
    )
    up_groups = grad_bias_up.reshape(FFH // group, group)
    up_zero = jnp.zeros_like(up_groups)
    grad_bias_up_full = jnp.where(
        is_zero,
        jnp.stack([up_groups, up_zero], axis=1),
        jnp.stack([up_zero, up_groups], axis=1),
    ).reshape(FF)
    grad_vector = jnp.concatenate(
        [
            spread(sums[0]),
            spread(sums[1]),
            grad_bias_out,
            grad_bias_up_full,
            grad_bias_out,
            grad_gain_one,
            grad_shift_one,
            grad_gain_two,
            grad_shift_two,
        ]
    )

    if staged:
        per = D // 32
        z, y, x = me >> 3, (me >> 2) & 1, ctx
        place = (z, y, x)
        dense_cols = [grad_dense[:, :HALF], grad_dense[:, HALF:]]
        keep = jnp.where(is_zero, dense_cols[0], dense_cols[1])
        got = swap(jnp.where(is_zero, dense_cols[1], dense_cols[0]), 2)
        dense_half = jnp.where(
            is_zero,
            jnp.concatenate([keep, got], axis=0),
            jnp.concatenate([got, keep], axis=0),
        )
        d6 = dense_half.reshape(4, 2, 2, 2, per, HALF)
        dn = grad_down.reshape(4, 2, 2, FF // 32, D)
        dense_wide = jnp.concatenate([d6[:, :, 0], d6[:, :, 1]], axis=-1)
        part_b = jnp.concatenate([dn[:, :, :, 64:], dense_wide], axis=3)
        done_d = scatter_pair(dn[:, :, :, :64], part_b.transpose(0, 2, 1, 3, 4), place)
        up6 = grad_up.reshape(4, 2, 2, 2, per, FFH)
        done_u = scatter_pair(up6[:, :, 0], up6[:, :, 1].transpose(0, 2, 1, 3, 4), place)
        lanes = jnp.pad(grad_vector.reshape(32, NVEC // 32), ((0, 0), (0, 384 - NVEC // 32)))
        lanes = jnp.pad(lanes.reshape(32, 3, 128), ((0, 0), (0, per - 3), (0, 0)))
        grad_q = jnp.concatenate([grad_qkv, lanes.reshape(D, 128)], axis=1)
        q6 = grad_q.reshape(4, 2, 2, 2, per, 3 * HALF + 128)
        done_q = scatter_pair(q6[:, :, 0], q6[:, :, 1].transpose(0, 2, 1, 3, 4), place)

        def core_swap(first, second):
            kept = jnp.where(is_zero, first, second)
            return kept, swap(jnp.where(is_zero, second, first), 2)

        def in_order(kept, got, axis):
            return jnp.where(
                is_zero,
                jnp.concatenate([kept, got], axis=axis),
                jnp.concatenate([got, kept], axis=axis),
            )

        q_keep, q_got = core_swap(done_q[:per], done_q[per:])
        u_keep, u_got = core_swap(done_u[:per], done_u[per:])
        e_keep, e_got = core_swap(
            done_d[FF // 32 :, :HALF], done_d[FF // 32 :, HALF:]
        )
        own_qkv = jnp.concatenate(
            [
                in_order(q_keep[:, HALF * j : HALF * j + HALF], q_got[:, HALF * j : HALF * j + HALF], 1)
                for j in range(3)
            ],
            axis=1,
        )
        own_vec = (q_keep[:3, 3 * HALF :] + q_got[:3, 3 * HALF :]).reshape(384)[: NVEC // 32]
        own_dense = in_order(e_keep, e_got, 1)
        three = lambda t: t.reshape(per, FFH // group, 1, group)
        own_up = in_order(three(u_keep), three(u_got), 2).reshape(per, FF)
        own_down = done_d[: FF // 32]
    else:
        widen = lambda t, axis: lax.dynamic_update_slice_in_dim(
            jnp.zeros(t.shape[:axis] + (2,) + t.shape[axis + 1 :], F32), t, core, axis
        )
        scatter = lambda t: lax.psum_scatter(t, AX, scatter_dimension=0, tiled=True)
        own_qkv = scatter(widen(grad_qkv.reshape(D, 3, 1, HALF), 2).reshape(D, 3 * D))
        own_dense = scatter(widen(grad_dense.reshape(1, HALF, D), 0).reshape(D, D))
        own_up = scatter(widen(grad_up.reshape(D, FFH // group, 1, group), 2).reshape(D, FF))
        own_down = scatter(widen(grad_down.reshape(FFH // group, 1, group, D), 1).reshape(FF, D))
        own_vec = scatter(grad_vector)

    grads = jnp.concatenate(
        [own_qkv.reshape(-1), own_dense.reshape(-1), own_up.reshape(-1), own_down.reshape(-1), own_vec]
    )
    squares = jnp.broadcast_to(jnp.sum(grads * grads), (8, 128))
    bit = 1
    while bit < owners:
        squares = squares + swap(squares, bit)
        bit *= 2
    new_params, new_first, new_second = adam_update(
        flat, grads, first_moment.reshape(-1), second_moment.reshape(-1), squares[0, 0]
    )

    partial_result = jnp.dot(att, dense_rows, preferred_element_type=F32) + jnp.dot(
        act, w_down, preferred_element_type=F32
    )
    result = (
        tokens.astype(F32)
        + partial_result[:rows]
        + swap(partial_result[rows:], 2)
        + (bias_dense + bias_down)
    ).astype(BF)
    gx = ga1 * gain_one + ga2 * gain_two
    gx_far = ga1f * gain_one
    far_total = gx_far[:rows] + swap(gx_far[rows:], 2)
    from_later = lax.ppermute(far_total.astype(BF), AX, [(i + 1, i) for i in range(0, owners, 2)])
    grad_normed = gx[:rows] + swap(gx[rows:], 2) + from_later.astype(F32)
    own_normed, own_inverse = normed[:rows], inverse[:rows]
    grad_inputs = cotangent + own_inverse * (
        grad_normed
        - jnp.mean(grad_normed, axis=1, keepdims=True)
        - own_normed * jnp.mean(grad_normed * own_normed, axis=1, keepdims=True)
    )
    row = lambda t: t.reshape(1, -1)
    return (result, grad_inputs, row(grads), row(new_params), row(new_first), row(new_second))


def solution(mesh):
    rows2 = P(AX, None)
    return jax.shard_map(
        on_device,
        mesh=mesh,
        in_specs=(rows2, rows2, P(AX), P(AX), rows2, rows2, rows2),
        out_specs=(rows2,) * 6,
        check_vma=False,
    )
```

time: 857 us -> 440 us (0.51)
  waiting for transfers between devices: 385 us -> 91.8 us
  matrix products: 225 us -> 48.4 us
  blocking collectives: 121 us -> 0 us
  starting transfers between devices: 14.8 us -> 91.5 us
  Pallas kernels: 0 us -> 56.9 us
  other arithmetic: 36.3 us -> 67.9 us
  local copies, waits for them, and re-layouts: 47.7 us -> 73 us
  between operations: 16 us -> 3.5 us
    reduce_scatter x4 -> x0, waiting for transfers between devices: 306 us -> none  [the longest x1 140 us: on_device(): lax.psum_scatter(grad_up, ('dp', 'ctx'), scatter_dimension=0, tiled=True)]
    dot_general x96 -> x15, matrix products: 225 us -> 48.4 us  [the longest x1 8.67 us: on_device(): jnp.dot(g_all, w_down.T, preferred_element_type=F32) * gelu_slope(pre)]
    unnamed x2 -> x0, blocking collectives: 80.8 us -> none
    ppermute x5 -> x62, starting transfers between devices: 14.2 us -> 91.5 us  [the longest x60 85.7 us: swap(): return lax.ppermute(value, AX, [(i, i ^ mask) for i in range(size)])]
    ppermute x5 -> x62, waiting for transfers between devices: 30.8 us -> 91.8 us  [the longest x60 81.9 us: swap(): return lax.ppermute(value, AX, [(i, i ^ mask) for i in range(size)])]
    pallas_call x0 -> x7, Pallas kernels: none -> 56.9 us  [the longest x1 19.2 us: attn_bwd(): pl.pallas_call(functools.partial(attn_bwd_kernel, rows), grid_spec=pltpu....]
    all_gather x4 -> x0, waiting for transfers between devices: 48 us -> none  [the longest x1 34.3 us: on_device(): lax.all_gather(shards[1], ('dp', 'ctx'), axis=0, tiled=True)]
    psum x1 -> x0, blocking collectives: 39.8 us -> none  [on_device(): squares_total = lax.psum(jnp.sum(grads * grads), ('dp', 'ctx'))]
  transfers between devices with their start and end apart: 13 -> 62, of which waited for: 7 -> 21; matrix products, arithmetic and copies ran while one was open for 34% -> 38% of each run, Pallas kernels for 0% -> 13%
where the time goes in v1:
time: 440 us; the launch traced here: 433 us
  waiting for transfers between devices  91.8 us (21%)
  starting transfers between devices  91.5 us (21%)
  local copies, waits for them, and re-layouts  73 us (17%)
  other arithmetic  67.9 us (15%)
  Pallas kernels  56.9 us (13%)
  matrix products  48.4 us (11%)
    ppermute x60, starting transfers between devices, swap(): return lax.ppermute(value, AX, [(i, i ^ mask) for i in range(size)])  85.7 us
    ppermute x60, waiting for transfers between devices, swap(): return lax.ppermute(value, AX, [(i, i ^ mask) for i in range(size)])  81.9 us
    unnamed x170, local copies, waits for them, and re-layouts  26.6 us
    pallas_call x1, Pallas kernels, attn_bwd(): pl.pallas_call(functools.partial(attn_bwd_kernel, rows), grid_spec=pltpu....  19.2 us
    pallas_call x1, Pallas kernels, attn_fwd(): pl.pallas_call(functools.partial(attn_fwd_kernel, rows), grid_spec=pltpu....  15.1 us
    pallas_call x3, Pallas kernels, assemble(): pl.pallas_call(kernel, out_shape=[jax.ShapeDtypeStruct(s, BF) for s in sh...  10.4 us
    ppermute x1, waiting for transfers between devices, on_device(): lax.ppermute(tokens, AX, [(i, i + 1) for i in range(0, owners, 2)])  9.88 us
  transfers between devices with their start and end apart: 62, of which 21 were waited for; matrix products, arithmetic and copies ran while one was open for 38% of the time, Pallas kernels for 13%

profile of v1, /device:TPU:0, one launch (start us, length us, event | category | flops | bytes accessed | tf_op | source)
XLA Modules:
  0.0 433.0 jit_solution(7468883121597194672)
XLA Ops:
  10.8 5.1 %bitcast_select_fusion = f32[128]{0:T(128)S(1)} fusion(f32[]{:T(128)} %bitcast.27, f32[]{:T(128)} %bitcast.28, f32[]{:T(128)} %bitcast.29, f32[]{:T(128)} %bitcast.30, f32[]{:T(128)} %bitcast.31, f32[]{:T(128)} %bitcast.33, f32[]{:T(128)} %bitcast.32, f32[]{:T(128)} %bitcast.26), kind=kLoop, calls=%fused_computation.310 | loop fusion | flops 4352 | bytes 544 | tf_op jit(solution)/shard_map/gather | solution.py:368
  18.3 5.7 %fusion.31 = (f32[1024,128]{1,0:T(8,128)}, f32[1024,128]{1,0:T(8,128)}, f32[1024,128]{1,0:T(8,128)}, f32[1024,128]{1,0:T(8,128)}, f32[1024,128]{1,0:T(8,128)}, /*index=5*/f32[1024,128]{1,0:T(8,128)}) fusion(f32[128]{0:T(128)S(1)} %bitcast_select_fusion, f32[1024]{0:T(1024)S(1)} %convert_element_type.278, pred[128]{0:T(512)(128)(4,1)S(1)} %get-tuple-element.173, ...), kind=kLoop, calls=%fused_computation.107 | loop fusion | flops 1310720 | bytes 3154816 | tf_op jit(solution)/shard_map/jit(_where)/select_n | solution.py:372
  25.7 4.1 collective-permute-start.4
  31.4 5.6 %collective-permute-done.4 = bf16[2,24,1280]{2,1,0:T(8,128)(2,1)S(1)} collective-permute-done((bf16[2,24,1280]{2,1,0:T(8,128)(2,1)S(1)}, bf16[2,24,1280]{2,1,0:T(8,128)(2,1)S(1)}, u32[]{:S(2)}, u32[]{:S(2)}) %collective-permute-start.4) | collective-permute-done | bytes 122912 | tf_op jit(solution)/shard_map/ppermute | solution.py:35
  36.9 4.1 collective-permute-start.20
  43.2 5.2 %collective-permute-done.21 = bf16[2,24,1536]{2,1,0:T(8,128)(2,1)S(1)} collective-permute-done((bf16[2,24,1536]{2,1,0:T(8,128)(2,1)S(1)}, bf16[2,24,1536]{2,1,0:T(8,128)(2,1)S(1)}, u32[]{:S(2)}, u32[]{:S(2)}) %collective-permute-start.21) | collective-permute-done | bytes 147488 | tf_op jit(solution)/shard_map/ppermute | solution.py:35
  48.5 10.4 %collective-permute-start.12 = (bf16[120,768]{1,0:T(8,128)(2,1)S(1)}, bf16[120,768]{1,0:T(8,128)(2,1)S(1)}, u32[]{:S(2)}, u32[]{:S(2)}) collective-permute-start(bf16[120,768]{1,0:T(8,128)(2,1)S(1)} %get-tuple-element.119), channel_id=1, source_target_pairs={{0,8},{1,9},{2,10},{3,11},{4,12},{5,13},{6,14},{7,15},{8,0},{9,1},... | collective-permute-start | bytes 552968 | tf_op jit(solution)/shard_map/ppermute | solution.py:35
  59.0 4.5 %collective-permute-start.8 = (bf16[4,1,24,1280]{3,2,1,0:T(8,128)(2,1)S(1)}, bf16[4,1,24,1280]{3,2,1,0:T(8,128)(2,1)S(1)}, u32[]{:S(2)}, u32[]{:S(2)}) collective-permute-start(bf16[4,1,24,1280]{3,2,1,0:T(8,128)(2,1)S(1)} %get-tuple-element.96), channel_id=1, source_target_pairs={{0,4},{1,5},{2,6},{3,7},{4,0},{5,1},{6,2},{7,3},{8,12},{9,13},{10,... | collective-permute-start | bytes 737288 | tf_op jit(solution)/shard_map/ppermute | solution.py:35
  65.0 5.9 %collective-permute-done.14 = bf16[120,768]{1,0:T(8,128)(2,1)S(1)} collective-permute-done((bf16[120,768]{1,0:T(8,128)(2,1)S(1)}, bf16[120,768]{1,0:T(8,128)(2,1)S(1)}, u32[]{:S(2)}, u32[]{:S(2)}) %collective-permute-start.14) | collective-permute-done | bytes 184352 | tf_op jit(solution)/shard_map/ppermute | solution.py:35
  74.9 4.6 %collective-permute-done.23 = bf16[4,1,24,1536]{3,2,0,1:T(8,128)(2,1)S(1)} collective-permute-done((bf16[4,1,24,1536]{3,2,0,1:T(8,128)(2,1)S(1)}, bf16[4,1,24,1536]{3,2,0,1:T(8,128)(2,1)S(1)}, u32[]{:S(2)}, u32[]{:S(2)}) %collective-permute-start.23) | collective-permute-done | bytes 294944 | tf_op jit(solution)/shard_map/ppermute | solution.py:35
  81.4 4.2 collective-permute-start.10
  96.8 9.9 %collective-permute-done.10 = bf16[512,768]{1,0:T(8,128)(2,1)} collective-permute-done((bf16[512,768]{1,0:T(8,128)(2,1)S(1)}, bf16[512,768]{1,0:T(8,128)(2,1)}, u32[]{:S(2)}, u32[]{:S(2)}) %collective-permute-start.10) | collective-permute-done | bytes 786464 | tf_op jit(solution)/shard_map/ppermute | solution.py:494
  112.9 4.3 collective-permute-done.9
  125.0 7.3 %shard_map.110 = (bf16[1024,384]{1,0:T(8,128)(2,1)}, bf16[1024,384]{1,0:T(8,128)(2,1)}, bf16[1024,384]{1,0:T(8,128)(2,1)}, bf16[1024,768]{1,0:T(8,128)(2,1)}, bf16[1024,768]{1,0:T(8,128)(2,1)}) custom-call(bf16[1024,768]{1,0:T(8,128)(2,1)} %copy-done, bf16[768,1280]{1,0:T(8,128)(2,1)} %bitcast.290, f32[8,768]{1,0:T(8,128)} %stack.177.vec_ref, ...), custom_call_target="tpu_custom_call" | custom-call | flops 1811939328 | bytes 8000000 | tf_op jit(solution)/shard_map/pallas_call | solution.py:167
  136.3 6.6 %multiply_convert_fusion = (bf16[1024,1536]{1,0:T(8,128)(2,1)S(1)}, f32[1024,1536]{1,0:T(8,128)}) fusion(f32[1536]{0:T(1024)S(1)} %add.374, bf16[1024,768]{1,0:T(8,128)(2,1)} %get-tuple-element.31, bf16[768,1536]{1,0:T(8,128)(2,1)} %bitcast.295), kind=kOutput, calls=%fused_computation.6 | convolution fusion | flops 2425356288 | bytes 13375488 | tf_op jit(solution)/shard_map/dot_general | solution.py:552
  158.9 8.7 %fusion.124 = (f32[1536]{0:T(1024)S(1)}, bf16[1024,1536]{1,0:T(8,128)(2,1)}) fusion(f32[1024,1536]{1,0:T(8,128)} %get-tuple-element.168, f32[1536]{0:T(1024)S(1)} %add.374, bf16[1024,768]{1,0:T(8,128)(2,1)S(1)} %constant_dynamic-update-slice_fusion.29, bf16[1536,768]{1,0:T(8,128)(2,1)} %bitcast.336), kind=kOutput, calls=%fused_computation.369 | convolution fusion | flops 2434791936 | bytes 13381632 | tf_op jit(solution)/shard_map/dot_general | solution.py:556
  168.4 5.0 %fusion.19 = f32[768,1536]{1,0:T(8,128)S(1)} fusion(bf16[1024,768]{1,0:T(8,128)(2,1)} %get-tuple-element.31, bf16[1024,1536]{1,0:T(8,128)(2,1)} %get-tuple-element.170), kind=kOutput, calls=%fused_computation.57 | convolution fusion | flops 2415919104 | bytes 9437184 | tf_op jit(solution)/shard_map/dot_general | solution.py:559
  178.1 4.2 fusion.125
  184.8 5.0 %shard_map.111 = (bf16[1024,384]{1,0:T(8,128)(2,1)}, bf16[1024,384]{1,0:T(8,128)(2,1)}, bf16[1024,768]{1,0:T(8,128)(2,1)}) custom-call(s32[1]{0:T(128)} %bitcast.35.used_ref, bf16[1024,768]{1,0:T(8,128)(2,1)} %copy-done.2, bf16[768,1280]{1,0:T(8,128)(2,1)} %bitcast.291, f32[8,768]{1,0:T(8,128)} %stack.177.vec_ref, f32[8,384]{1,0:T(8,128)} %maximum_maximum_fusion.2.bias_ref, ...), custom_call_target="tpu_custom_call" | custom-call | flops 1811939328 | bytes 8000000 | tf_op jit(solution)/shard_map/pallas_call | solution.py:175
  189.7 15.1 %shard_map.112 = (bf16[1024,384]{1,0:T(8,128)(2,1)}, f32[1024,384]{1,0:T(8,128)}) custom-call(s32[4]{0:T(128)} %fusion.101.plan_ref, bf16[1024,384]{1,0:T(8,128)(2,1)} %get-tuple-element.24.q_ref, bf16[1024,384]{1,0:T(8,128)(2,1)} %get-tuple-element.25.k_ref, bf16[1024,384]{1,0:T(8,128)(2,1)} %get-tuple-element.26.v_ref, ...), custom_call_target="tpu_custom_call" | custom-call | flops 20000000000 | bytes 6000000 | tf_op jit(solution)/shard_map/pallas_call | solution.py:323
  216.5 19.2 %shard_map.115 = (bf16[1024,384]{1,0:T(8,128)(2,1)}, bf16[1024,384]{1,0:T(8,128)(2,1)}, bf16[1024,384]{1,0:T(8,128)(2,1)}, bf16[1024,384]{1,0:T(8,128)(2,1)}, bf...) custom-call(s32[4]{0:T(128)} %fusion.101.plan_ref, bf16[1024,384]{1,0:T(8,128)(2,1)} %get-tuple-element.24.q_ref, ...), custom_call_target="tpu_custom_call" | custom-call | flops 40000000000 | bytes 10000000 | tf_op jit(solution)/shard_map/pallas_call | solution.py:346
  246.9 5.2 %fusion.110 = (f32[768]{0:T(1024)}, f32[768]{0:T(1024)}, f32[1024,768]{1,0:T(8,128)S(1)}, f32[768]{0:T(1024)}, f32[768]{0:T(1024)}, /*index=5*/f32[1024,768]{1,0:T(8,128)}) fusion(f32[1024]{0:T(1024)S(1)} %copy-done.52, f32[1024]{0:T(1024)S(1)} %broadcast_multiply_fusion.2, bf16[1024,768]{1,0:T(8,128)(2,1)S(1)} %copy-done.1, ...), kind=kOutput, calls=%fused_computation.357 | convolution fusion | flops 2425353216 | bytes 16541696 | tf_op jit(solution)/shard_map/dot_general | solution.py:580
  280.5 6.0 %collective-permute-start.54 = (bf16[48,1536]{1,0:T(8,128)(2,1)S(1)}, bf16[48,1536]{1,0:T(8,128)(2,1)S(1)}, u32[]{:S(2)}, u32[]{:S(2)}) collective-permute-start(bf16[48,1536]{1,0:T(8,128)(2,1)S(1)} %get-tuple-element.71), channel_id=1, source_target_pairs={{0,16},{1,17},{2,18},{3,19},{4,20},{5,21},{6,22},{7,23},{8,24},{9,... | collective-permute-start | bytes 442376 | tf_op jit(solution)/shard_map/ppermute | solution.py:35
  286.7 10.5 %collective-permute-done.54 = bf16[48,1536]{1,0:T(8,128)(2,1)S(1)} collective-permute-done((bf16[48,1536]{1,0:T(8,128)(2,1)S(1)}, bf16[48,1536]{1,0:T(8,128)(2,1)S(1)}, u32[]{:S(2)}, u32[]{:S(2)}) %collective-permute-start.54) | collective-permute-done | bytes 147488 | tf_op jit(solution)/shard_map/ppermute | solution.py:35
  297.9 6.8 %collective-permute-done.44 = bf16[4,56,768]{2,1,0:T(8,128)(2,1)S(1)} collective-permute-done((bf16[4,56,768]{2,1,0:T(8,128)(2,1)S(1)}, bf16[4,56,768]{2,1,0:T(8,128)(2,1)S(1)}, u32[]{:S(2)}, u32[]{:S(2)}) %collective-permute-start.44) | collective-permute-done | bytes 344096 | tf_op jit(solution)/shard_map/ppermute | solution.py:35
  322.3 4.7 %collective-permute-done.46 = bf16[120,768]{1,0:T(8,128)(2,1)} collective-permute-done((bf16[120,768]{1,0:T(8,128)(2,1)}, bf16[120,768]{1,0:T(8,128)(2,1)}, u32[]{:S(2)}, u32[]{:S(2)}) %collective-permute-start.46) | collective-permute-done | bytes 184352 | tf_op jit(solution)/shard_map/ppermute | solution.py:35
  365.0 5.1 %collective-permute-done.32 = bf16[4,2,24,1280]{3,2,0,1:T(8,128)(2,1)} collective-permute-done((bf16[4,2,24,1280]{3,2,0,1:T(8,128)(2,1)}, bf16[4,2,24,1280]{3,2,0,1:T(8,128)(2,1)}, u32[]{:S(2)}, u32[]{:S(2)}) %collective-permute-start.32) | collective-permute-done | bytes 491552 | tf_op jit(solution)/shard_map/ppermute | solution.py:35
  372.5 5.8 %collective-permute-done.34 = bf16[4,2,24,1280]{3,2,1,0:T(8,128)(2,1)S(1)} collective-permute-done((bf16[4,2,24,1280]{3,2,1,0:T(8,128)(2,1)S(1)}, bf16[4,2,24,1280]{3,2,1,0:T(8,128)(2,1)S(1)}, u32[]{:S(2)}, u32[]{:S(2)}) %collective-permute-start.34) | collective-permute-done | bytes 491552 | tf_op jit(solution)/shard_map/ppermute | solution.py:35
  378.5 4.3 collective-permute-done.33
  393.3 4.9 %collective-permute-done.37 = bf16[48,1280]{1,0:T(8,128)(2,1)S(1)} collective-permute-done((bf16[48,1280]{1,0:T(8,128)(2,1)S(1)}, bf16[48,1280]{1,0:T(8,128)(2,1)S(1)}, u32[]{:S(2)}, u32[]{:S(2)}) %collective-permute-start.37) | collective-permute-done | bytes 122912 | tf_op jit(solution)/shard_map/ppermute | solution.py:35
  418.6 5.2 %reshape.728 = f32[1,221472]{1,0:T(1,128)} reshape(f32[221472]{0:T(1024)S(1)} %get-tuple-element.154) | data formatting | bytes 1771776 | tf_op jit(solution)/shard_map/reshape | solution.py:710
  425.0 7.5 %multiply_subtract_fusion = (f32[1,221472]{1,0:T(1,128)}, f32[1,221472]{1,0:T(1,128)}, f32[1,221472]{1,0:T(1,128)}) fusion(f32[1,221472]{1,0:T(1,128)S(1)} %copy-done.17, f32[1,221472]{1,0:T(1,128)S(1)} %constant_dynamic-update-slice_fusion.37, f32[]{:T(128)} %bitcast.115, f32[1,221472]{1,0:T(1,128)S(1)} %copy-done.35, f32[1,221472]{1,0:T(1,128)S(1)} %copy-done.36), kind=kLoop, calls=%fused_computation.96 | loop fusion | flops 3543552 | bytes 6201220 | tf_op jit(solution)/shard_map/sub | solution.py:400
  (475 shorter events, 219.1 us)
Async XLA Ops:
  0.6 16.3 %collective-permute-start = (s32[512]{0:T(512)}, s32[512]{0:T(512)S(1)}, u32[]{:S(2)}, u32[]{:S(2)}) collective-permute-start(s32[512]{0:T(512)} %param.9), channel_id=1, source_target_pairs={{0,2},{1,3},{2,0},{3,1},{4,6},{5,7},{6,4},{7,5},{8,10},{9,11},{10,... | collective-permute-start | bytes 6152 | tf_op jit(solution)/shard_map/ppermute | solution.py:35
  1.2 107.9 %collective-permute-start.28 = (bf16[512,768]{1,0:T(8,128)(2,1)}, bf16[512,768]{1,0:T(8,128)(2,1)}, u32[]{:S(2)}, u32[]{:S(2)}) collective-permute-start(bf16[512,768]{1,0:T(8,128)(2,1)} %param.8), channel_id=1, source_target_pairs={{0,2},{1,3},{2,0},{3,1},{4,6},{5,7},{6,4},{7,5},{8,10},{9,11},{10,... | collective-permute-start | bytes 2359304 | tf_op jit(solution)/shard_map/ppermute | solution.py:35
  1.3 91.9 %collective-permute-start.1 = (bf16[512,768]{1,0:T(8,128)(2,1)}, bf16[512,768]{1,0:T(8,128)(2,1)}, u32[]{:S(2)}, u32[]{:S(2)}) collective-permute-start(bf16[512,768]{1,0:T(8,128)(2,1)} %param.7), channel_id=1, source_target_pairs={{0,2},{1,3},{2,0},{3,1},{4,6},{5,7},{6,4},{7,5},{8,10},{9,11},{10,... | collective-permute-start | bytes 2359304 | tf_op jit(solution)/shard_map/ppermute | solution.py:35
  7.7 16.8 %collective-permute-start.2 = (bf16[24,3200]{1,0:T(8,128)(2,1)}, bf16[24,3200]{1,0:T(8,128)(2,1)}, u32[]{:S(2)}, u32[]{:S(2)}) collective-permute-start(bf16[24,3200]{1,0:T(8,128)(2,1)} %broadcast_select_fusion), channel_id=1, source_target_pairs={{0,2},{1,3},{2,0},{3,1},{4,6},{5,7},{6,4},{7,5},{8,10},{9,11},{10,... | collective-permute-start | bytes 460808 | tf_op jit(solution)/shard_map/ppermute | solution.py:35
  41.0 17.8 %collective-permute-start.22 = (bf16[2,24,1536]{2,1,0:T(8,128)(2,1)S(1)}, bf16[2,24,1536]{2,1,0:T(8,128)(2,1)S(1)}, u32[]{:S(2)}, u32[]{:S(2)}) collective-permute-start(bf16[2,24,1536]{2,1,0:T(8,128)(2,1)S(1)} %get-tuple-element.107), channel_id=1, source_target_pairs={{0,24},{1,25},{2,26},{3,27},{4,28},{5,29},{6,30},{7,31},{8,16},{9,... | collective-permute-start | bytes 442376 | tf_op jit(solution)/shard_map/ppermute | solution.py:35
  48.5 15.4 %collective-permute-start.12 = (bf16[120,768]{1,0:T(8,128)(2,1)S(1)}, bf16[120,768]{1,0:T(8,128)(2,1)S(1)}, u32[]{:S(2)}, u32[]{:S(2)}) collective-permute-start(bf16[120,768]{1,0:T(8,128)(2,1)S(1)} %get-tuple-element.119), channel_id=1, source_target_pairs={{0,8},{1,9},{2,10},{3,11},{4,12},{5,13},{6,14},{7,15},{8,0},{9,1},... | collective-permute-start | bytes 552968 | tf_op jit(solution)/shard_map/ppermute | solution.py:35
  59.0 14.2 %collective-permute-start.8 = (bf16[4,1,24,1280]{3,2,1,0:T(8,128)(2,1)S(1)}, bf16[4,1,24,1280]{3,2,1,0:T(8,128)(2,1)S(1)}, u32[]{:S(2)}, u32[]{:S(2)}) collective-permute-start(bf16[4,1,24,1280]{3,2,1,0:T(8,128)(2,1)S(1)} %get-tuple-element.96), channel_id=1, source_target_pairs={{0,4},{1,5},{2,6},{3,7},{4,0},{5,1},{6,2},{7,3},{8,12},{9,13},{10,... | collective-permute-start | bytes 737288 | tf_op jit(solution)/shard_map/ppermute | solution.py:35
  81.4 25.2 %collective-permute-start.10 = (bf16[512,768]{1,0:T(8,128)(2,1)S(1)}, bf16[512,768]{1,0:T(8,128)(2,1)}, u32[]{:S(2)}, u32[]{:S(2)}) collective-permute-start(bf16[512,768]{1,0:T(8,128)(2,1)S(1)} %copy-done.26), channel_id=1, source_target_pairs={{0,1},{2,3},{4,5},{6,7},{8,9},{10,11},{12,13},{14,15},{16,17},{18,... | collective-permute-start | bytes 2359304 | tf_op jit(solution)/shard_map/ppermute | solution.py:494
  86.8 30.5 %collective-permute-start.9 = (bf16[2,4,1,24,1280]{4,3,1,2,0:T(8,128)(2,1)S(1)}, bf16[2,4,1,24,1280]{4,3,1,2,0:T(8,128)(2,1)S(1)}, u32[]{:S(2)}, u32[]{:S(2)}) collective-permute-start(bf16[2,4,1,24,1280]{4,3,1,2,0:T(8,128)(2,1)S(1)} %get-tuple-element.92), channel_id=1, source_target_pairs={{0,1},{1,0},{2,3},{3,2},{4,5},{5,4},{6,7},{7,6},{8,9},{9,8},{10,11... | collective-permute-start | bytes 1474568 | tf_op jit(solution)/shard_map/ppermute | solution.py:35
  90.4 28.0 %collective-permute-start.7 = (bf16[2,4,1,24,1280]{4,3,1,2,0:T(8,128)(2,1)S(1)}, bf16[2,4,1,24,1280]{4,3,1,2,0:T(8,128)(2,1)S(1)}, u32[]{:S(2)}, u32[]{:S(2)}) collective-permute-start(bf16[2,4,1,24,1280]{4,3,1,2,0:T(8,128)(2,1)S(1)} %get-tuple-element.98), channel_id=1, source_target_pairs={{0,4},{1,5},{2,6},{3,7},{4,0},{5,1},{6,2},{7,3},{8,12},{9,13},{10,... | collective-permute-start | bytes 1474568 | tf_op jit(solution)/shard_map/ppermute | solution.py:35
  93.2 39.7 %collective-permute-start.26 = (bf16[2,4,1,24,1536]{4,3,1,0,2:T(8,128)(2,1)}, bf16[2,4,1,24,1536]{4,3,1,0,2:T(8,128)(2,1)}, u32[]{:S(2)}, u32[]{:S(2)}) collective-permute-start(bf16[2,4,1,24,1536]{4,3,1,0,2:T(8,128)(2,1)} %get-tuple-element.84), channel_id=1, source_target_pairs={{0,1},{1,0},{2,3},{3,2},{4,5},{5,4},{6,7},{7,6},{8,9},{9,8},{10,11... | collective-permute-start | bytes 1769480 | tf_op jit(solution)/shard_map/ppermute | solution.py:35
  106.7 26.2 %collective-permute-start.24 = (bf16[2,4,1,24,1536]{4,3,1,2,0:T(8,128)(2,1)}, bf16[2,4,1,24,1536]{4,3,1,2,0:T(8,128)(2,1)}, u32[]{:S(2)}, u32[]{:S(2)}) collective-permute-start(bf16[2,4,1,24,1536]{4,3,1,2,0:T(8,128)(2,1)} %get-tuple-element.90), channel_id=1, source_target_pairs={{0,4},{1,5},{2,6},{3,7},{4,0},{5,1},{6,2},{7,3},{8,12},{9,13},{10,... | collective-permute-start | bytes 1769480 | tf_op jit(solution)/shard_map/ppermute | solution.py:35
  109.1 44.0 %collective-permute-start.18 = (bf16[2,4,56,768]{3,2,1,0:T(8,128)(2,1)}, bf16[2,4,56,768]{3,2,1,0:T(8,128)(2,1)}, u32[]{:S(2)}, u32[]{:S(2)}) collective-permute-start(bf16[2,4,56,768]{3,2,1,0:T(8,128)(2,1)} %pad_maximum_fusion.3.b8), channel_id=1, source_target_pairs={{0,1},{1,0},{2,3},{3,2},{4,5},{5,4},{6,7},{7,6},{8,9},{9,8},{10,11... | collective-permute-start | bytes 2064392 | tf_op jit(solution)/shard_map/ppermute | solution.py:35
  117.2 35.9 %collective-permute-start.16 = (bf16[2,4,64,768]{3,2,1,0:T(8,128)(2,1)}, bf16[2,4,64,768]{3,2,1,0:T(8,128)(2,1)}, u32[]{:S(2)}, u32[]{:S(2)}) collective-permute-start(bf16[2,4,64,768]{3,2,1,0:T(8,128)(2,1)} %pad_maximum_fusion.1.a8), channel_id=1, source_target_pairs={{0,4},{1,5},{2,6},{3,7},{4,0},{5,1},{6,2},{7,3},{8,12},{9,13},{10,... | collective-permute-start | bytes 2359304 | tf_op jit(solution)/shard_map/ppermute | solution.py:35
  118.4 63.9 %collective-permute-start.11 = (bf16[512,768]{1,0:T(8,128)(2,1)}, bf16[512,768]{1,0:T(8,128)(2,1)}, u32[]{:S(2)}, u32[]{:S(2)}) collective-permute-start(bf16[512,768]{1,0:T(8,128)(2,1)} %collective-permute-done.10), channel_id=1, source_target_pairs={{0,2},{1,3},{2,0},{3,1},{4,6},{5,7},{6,4},{7,5},{8,10},{9,11},{10,... | collective-permute-start | bytes 2359304 | tf_op jit(solution)/shard_map/ppermute | solution.py:35
  150.6 59.5 %collective-permute-start.40 = (bf16[4,2,64,768]{3,2,0,1:T(8,128)(2,1)}, bf16[4,2,64,768]{3,2,0,1:T(8,128)(2,1)}, u32[]{:S(2)}, u32[]{:S(2)}) collective-permute-start(bf16[4,2,64,768]{3,2,0,1:T(8,128)(2,1)} %fusion.30), channel_id=1, source_target_pairs={{0,1},{1,0},{2,3},{3,2},{4,5},{5,4},{6,7},{7,6},{8,9},{9,8},{10,11... | collective-permute-start | bytes 2359304 | tf_op jit(solution)/shard_map/ppermute | solution.py:35
  158.9 54.2 %collective-permute-start.19 = (bf16[768,384]{1,0:T(8,128)(2,1)}, bf16[768,384]{1,0:T(8,128)(2,1)}, u32[]{:S(2)}, u32[]{:S(2)}) collective-permute-start(bf16[768,384]{1,0:T(8,128)(2,1)} %bitcast.49), channel_id=1, source_target_pairs={{0,2},{1,3},{2,0},{3,1},{4,6},{5,7},{6,4},{7,5},{8,10},{9,11},{10,... | collective-permute-start | bytes 1769480 | tf_op jit(solution)/shard_map/ppermute | solution.py:35
  174.9 83.6 %collective-permute-start.49 = (bf16[4,2,24,1536]{3,2,0,1:T(8,128)(2,1)}, bf16[4,2,24,1536]{3,2,0,1:T(8,128)(2,1)}, u32[]{:S(2)}, u32[]{:S(2)}) collective-permute-start(bf16[4,2,24,1536]{3,2,0,1:T(8,128)(2,1)} %fusion.37), channel_id=1, source_target_pairs={{0,1},{1,0},{2,3},{3,2},{4,5},{5,4},{6,7},{7,6},{8,9},{9,8},{10,11... | collective-permute-start | bytes 1769480 | tf_op jit(solution)/shard_map/ppermute | solution.py:35
  175.8 86.8 %collective-permute-start.51 = (bf16[4,2,24,1536]{3,2,1,0:T(8,128)(2,1)}, bf16[4,2,24,1536]{3,2,1,0:T(8,128)(2,1)}, u32[]{:S(2)}, u32[]{:S(2)}) collective-permute-start(bf16[4,2,24,1536]{3,2,1,0:T(8,128)(2,1)} %fusion.36), channel_id=1, source_target_pairs={{0,4},{1,5},{2,6},{3,7},{4,0},{5,1},{6,2},{7,3},{8,12},{9,13},{10,... | collective-permute-start | bytes 1769480 | tf_op jit(solution)/shard_map/ppermute | solution.py:35
  208.0 63.8 %collective-permute-start.42 = (f32[384,384]{1,0:T(8,128)}, f32[384,384]{1,0:T(8,128)}, u32[]{:S(2)}, u32[]{:S(2)}) collective-permute-start(f32[384,384]{1,0:T(8,128)} %get-tuple-element.76), channel_id=1, source_target_pairs={{0,2},{1,3},{2,0},{3,1},{4,6},{5,7},{6,4},{7,5},{8,10},{9,11},{10,... | collective-permute-start | bytes 1769480 | tf_op jit(solution)/shard_map/ppermute | solution.py:35
  212.4 74.1 %collective-permute-start.41 = (bf16[4,64,768]{2,1,0:T(8,128)(2,1)}, bf16[4,64,768]{2,1,0:T(8,128)(2,1)S(1)}, u32[]{:S(2)}, u32[]{:S(2)}) collective-permute-start(bf16[4,64,768]{2,1,0:T(8,128)(2,1)} %fusion.48), channel_id=1, source_target_pairs={{0,4},{1,5},{2,6},{3,7},{4,0},{5,1},{6,2},{7,3},{8,12},{9,13},{10,... | collective-permute-start | bytes 1179656 | tf_op jit(solution)/shard_map/ppermute | solution.py:35
  242.8 62.1 %collective-permute-start.30 = (f32[512,768]{1,0:T(8,128)S(1)}, f32[512,768]{1,0:T(8,128)S(1)}, u32[]{:S(2)}, u32[]{:S(2)}) collective-permute-start(f32[512,768]{1,0:T(8,128)S(1)} %slice.389), channel_id=1, source_target_pairs={{0,2},{1,3},{2,0},{3,1},{4,6},{5,7},{6,4},{7,5},{8,10},{9,11},{10,... | collective-permute-start | bytes 4718600 | tf_op jit(solution)/shard_map/ppermute | solution.py:35
  259.7 16.6 %collective-permute-start.50 = (bf16[4,24,1536]{2,1,0:T(8,128)(2,1)S(1)}, bf16[4,24,1536]{2,1,0:T(8,128)(2,1)S(1)}, u32[]{:S(2)}, u32[]{:S(2)}) collective-permute-start(bf16[4,24,1536]{2,1,0:T(8,128)(2,1)S(1)} %fusion.61), channel_id=1, source_target_pairs={{0,4},{1,5},{2,6},{3,7},{4,0},{5,1},{6,2},{7,3},{8,12},{9,13},{10,... | collective-permute-start | bytes 884744 | tf_op jit(solution)/shard_map/ppermute | solution.py:35
  275.1 22.1 %collective-permute-start.43 = (bf16[4,2,56,768]{3,2,0,1:T(8,128)(2,1)S(1)}, bf16[4,2,56,768]{3,2,0,1:T(8,128)(2,1)S(1)}, u32[]{:S(2)}, u32[]{:S(2)}) collective-permute-start(bf16[4,2,56,768]{3,2,0,1:T(8,128)(2,1)S(1)} %fusion.35), channel_id=1, source_target_pairs={{0,4},{1,5},{2,6},{3,7},{4,0},{5,1},{6,2},{7,3},{8,12},{9,13},{10,... | collective-permute-start | bytes 2064392 | tf_op jit(solution)/shard_map/ppermute | solution.py:35
  280.5 16.7 %collective-permute-start.54 = (bf16[48,1536]{1,0:T(8,128)(2,1)S(1)}, bf16[48,1536]{1,0:T(8,128)(2,1)S(1)}, u32[]{:S(2)}, u32[]{:S(2)}) collective-permute-start(bf16[48,1536]{1,0:T(8,128)(2,1)S(1)} %get-tuple-element.71), channel_id=1, source_target_pairs={{0,16},{1,17},{2,18},{3,19},{4,20},{5,21},{6,22},{7,23},{8,24},{9,... | collective-permute-start | bytes 442376 | tf_op jit(solution)/shard_map/ppermute | solution.py:35
  286.6 42.4 %collective-permute-start.29 = (f32[512,768]{1,0:T(8,128)}, f32[512,768]{1,0:T(8,128)}, u32[]{:S(2)}, u32[]{:S(2)}) collective-permute-start(f32[512,768]{1,0:T(8,128)} %slice.387), channel_id=1, source_target_pairs={{0,2},{1,3},{2,0},{3,1},{4,6},{5,7},{6,4},{7,5},{8,10},{9,11},{10,... | collective-permute-start | bytes 4718600 | tf_op jit(solution)/shard_map/ppermute | solution.py:35
  297.9 15.8 %collective-permute-start.56 = (f32[24,1536]{1,0:T(8,128)S(1)}, f32[24,1536]{1,0:T(8,128)S(1)}, u32[]{:S(2)}, u32[]{:S(2)}) collective-permute-start(f32[24,1536]{1,0:T(8,128)S(1)} %get-tuple-element.111), channel_id=1, source_target_pairs={{0,2},{1,3},{2,0},{3,1},{4,6},{5,7},{6,4},{7,5},{8,10},{9,11},{10,... | collective-permute-start | bytes 442376 | tf_op jit(solution)/shard_map/ppermute | solution.py:35
  306.0 23.0 %collective-permute-start.31 = (bf16[512,768]{1,0:T(8,128)(2,1)}, bf16[512,768]{1,0:T(8,128)(2,1)}, u32[]{:S(2)}, u32[]{:S(2)}) collective-permute-start(bf16[512,768]{1,0:T(8,128)(2,1)} %fusion.13), channel_id=1, source_target_pairs={{1,0},{3,2},{5,4},{7,6},{9,8},{11,10},{13,12},{15,14},{17,16},{19,... | collective-permute-start | bytes 2359304 | tf_op jit(solution)/shard_map/ppermute | solution.py:702
  311.5 15.5 %collective-permute-start.46 = (bf16[120,768]{1,0:T(8,128)(2,1)}, bf16[120,768]{1,0:T(8,128)(2,1)}, u32[]{:S(2)}, u32[]{:S(2)}) collective-permute-start(bf16[120,768]{1,0:T(8,128)(2,1)} %get-tuple-element.68), channel_id=1, source_target_pairs={{0,16},{1,17},{2,18},{3,19},{4,20},{5,21},{6,22},{7,23},{8,24},{9,... | collective-permute-start | bytes 552968 | tf_op jit(solution)/shard_map/ppermute | solution.py:35
  322.3 68.3 %collective-permute-start.27 = (f32[512,768]{1,0:T(8,128)}, f32[512,768]{1,0:T(8,128)}, u32[]{:S(2)}, u32[]{:S(2)}) collective-permute-start(f32[512,768]{1,0:T(8,128)} %slice.381), channel_id=1, source_target_pairs={{0,2},{1,3},{2,0},{3,1},{4,6},{5,7},{6,4},{7,5},{8,10},{9,11},{10,... | collective-permute-start | bytes 4718600 | tf_op jit(solution)/shard_map/ppermute | solution.py:35
  328.9 31.8 %collective-permute-start.48 = (f32[24,384]{1,0:T(8,128)}, f32[24,384]{1,0:T(8,128)}, u32[]{:S(2)}, u32[]{:S(2)}) collective-permute-start(f32[24,384]{1,0:T(8,128)} %get-tuple-element.103), channel_id=1, source_target_pairs={{0,2},{1,3},{2,0},{3,1},{4,6},{5,7},{6,4},{7,5},{8,10},{9,11},{10,... | collective-permute-start | bytes 110600 | tf_op jit(solution)/shard_map/ppermute | solution.py:35
  354.7 15.4 %collective-permute-start.32 = (bf16[4,2,24,1280]{3,2,0,1:T(8,128)(2,1)}, bf16[4,2,24,1280]{3,2,0,1:T(8,128)(2,1)}, u32[]{:S(2)}, u32[]{:S(2)}) collective-permute-start(bf16[4,2,24,1280]{3,2,0,1:T(8,128)(2,1)} %fusion.47), channel_id=1, source_target_pairs={{0,1},{1,0},{2,3},{3,2},{4,5},{5,4},{6,7},{7,6},{8,9},{9,8},{10,11... | collective-permute-start | bytes 1474568 | tf_op jit(solution)/shard_map/ppermute | solution.py:35
  (96 other events, 612.6 us)

commit v2 on v1

--- a/solution.py
+++ b/solution.py
@@ -39,17 +39,33 @@
     return lax.dynamic_index_in_dim(value, index, axis, keepdims=False)
 
 
-def gather_pair(both, rows_a):
-    z_all = jnp.stack([both, swap(both, 8), swap(both, 16), swap(both, 24)])
+def gather_pair(both, rows_a, after=None):
+    got = [swap(both, 8), swap(both, 16), swap(both, 24)]
+    z_all = jnp.stack([both] + got)
     part_a, part_b = z_all[:, :rows_a], z_all[:, rows_a:]
     eight_a = jnp.stack([part_a, swap(part_a, 1)])
     eight_b = jnp.stack([part_b, swap(part_b, 4)])
-    return eight_a, swap(eight_a, 4), eight_b, swap(eight_b, 1)
-
-
-def rel_places(me, rel_z, rel_y, rel_x):
-    outer = lax.shift_right_logical(me, 2)
-    return outer ^ (rel_z * 2 + rel_y), (me & 1) ^ rel_x
+    return (eight_a, swap(eight_a, 4), eight_b, swap(eight_b, 1)), got[2]
+
+
+def whole(shape):
+    return pl.BlockSpec(shape, lambda *_: (0,) * len(shape))
+
+
+SMEM = pl.BlockSpec(memory_space=pltpu.SMEM)
+VMEM = pl.BlockSpec(memory_space=pltpu.VMEM)
+HBM = pl.BlockSpec(memory_space=pl.ANY)
+
+
+def local_call(kernel, place, inputs, outs, scratch=(), in_specs=None, size=4_000_000):
+    return pl.pallas_call(
+        kernel,
+        out_shape=[jax.ShapeDtypeStruct(shape, kind) for shape, kind in outs],
+        in_specs=[SMEM] + (in_specs or [VMEM] * len(inputs)),
+        out_specs=[VMEM] * len(outs),
+        scratch_shapes=list(scratch),
+        cost_estimate=pl.CostEstimate(flops=0, bytes_accessed=size, transcendentals=0),
+    )(place, *inputs)
 
 
 def copy_all(copies):
@@ -59,53 +75,361 @@
         one.wait()
 
 
-def assemble_pair_kernel(me_ref, a8, ay, b8, bx, out, sems):
-    me = me_ref[0]
-    copies = []
+LANES = 128
+AT_DENSE, AT_UP, AT_DOWN, AT_VEC, AT_END = 432, 576, 1152, 1728, 1736
+NPAR = AT_VEC * LANES + 288
+
+
+def flat_to_rows(flat_ref, rows_ref):
+    for k in range(AT_VEC // 8):
+        rows_ref[8 * k : 8 * k + 8, :] = flat_ref[0:1, 1024 * k : 1024 * k + 1024].reshape(8, 128)
+
+
+def half_tiles(tiles, core):
+    lane = lax.broadcasted_iota(jnp.int32, tiles[0].shape, 1)
+    roll = lambda t: pltpu.roll(t, 64, 1)
+    mix = lambda first, second: jnp.where(lane < 64, first, second)
+    out = []
+    for k in range(4):
+        t0, t1, t2, u0, u1, u2 = tiles[6 * k : 6 * k + 6]
+        if core == 0:
+            out += [t0, mix(t1, roll(u0)), mix(roll(u0), roll(u1))]
+        else:
+            out += [mix(roll(t1), roll(t2)), mix(roll(t2), u1), u2]
+    return out
+
+
+def full_tiles(first, second):
+    lane = lax.broadcasted_iota(jnp.int32, first[0].shape, 1)
+    roll = lambda t: pltpu.roll(t, 64, 1)
+    mix = lambda a, b: jnp.where(lane < 64, a, b)
+    out = []
+    for k in range(4):
+        a0, a1, a2 = first[3 * k : 3 * k + 3]
+        b0, b1, b2 = second[3 * k : 3 * k + 3]
+        out += [a0, mix(a1, roll(b0)), mix(roll(b0), roll(b1))]
+        out += [mix(roll(a1), roll(a2)), mix(roll(a2), b1), b2]
+    return out
+
+
+def prep_kernel(place_ref, flat_ref, mine_ref, other_ref, down_ref, rows_ref):
+    flat_to_rows(flat_ref, rows_ref)
+    is_zero = place_ref[3] == 0
+    base = AT_VEC * LANES
+    zero = jnp.zeros((8, 128), F32)
+    rows_ref[AT_VEC : AT_VEC + 8, :] = zero
+    for k in range(2):
+        rows_ref[AT_VEC + k : AT_VEC + k + 1, :] = flat_ref[0:1, base + 128 * k : base + 128 * k + 128]
+    rows_ref[AT_VEC + 2 : AT_VEC + 3, 0:32] = flat_ref[0:1, base + 256 : base + 288]
+    for b in range(3):
+        span = slice(8 * b, 8 * b + 8)
+        tile = lambda start, per, t: rows_ref[pl.ds(start + 8 * per * b + t, 8, stride=per), :]
+        ups = [tile(AT_UP, 24, t) for t in range(24)]
+        sets = []
+        for c in range(2):
+            tiles = [tile(0, 18, 6 * j + 3 * c + u) for j in range(3) for u in range(3)]
+            tiles.append(rows_ref[AT_VEC : AT_VEC + 8, :] if b == 0 else zero)
+            tiles += half_tiles(ups, c)
+            tiles += [tile(AT_DENSE, 6, 3 * c + u) for u in range(3)]
+            sets.append(tiles)
+        for t in range(25):
+            at = slice(128 * t, 128 * t + 128)
+            mine_ref[span, at] = jnp.where(is_zero, sets[0][t], sets[1][t]).astype(BF)
+            other_ref[span, at] = jnp.where(is_zero, sets[1][t], sets[0][t]).astype(BF)
+    for b in range(12):
+        for t in range(6):
+            down_ref[8 * b : 8 * b + 8, 128 * t : 128 * t + 128] = rows_ref[
+                pl.ds(AT_DOWN + 48 * b + t, 8, stride=6), :
+            ].astype(BF)
+
+
+Q_END, U_END, PACK = 1280, 2816, 3200
+ROWS_A = 96
+
+
+def regroup_q_kernel(place_ref, mine_ref, got_ref, q_ref):
+    core = place_ref[3]
+    q_ref[core] = mine_ref[:, :Q_END]
+    q_ref[1 - core] = got_ref[:, :Q_END]
+
+
+def regroup_ud_kernel(place_ref, mine_ref, got_ref, down_ref, after_ref, out_ref):
+    del after_ref
+    is_zero = place_ref[3] == 0
+    for c in range(2):
+        first, second = (mine_ref, got_ref) if c == 0 else (got_ref, mine_ref)
+        take = lambda lo, hi: jnp.where(is_zero, first[:, lo:hi], second[:, lo:hi])
+        for h in range(2):
+            at = 24 * (2 * c + h)
+            out_ref[at : at + 24, :] = take(Q_END + 768 * h, Q_END + 768 * h + 768)
+        out_ref[192:216, 384 * c : 384 * c + 384] = take(U_END, PACK)
+    out_ref[96:192, :] = down_ref[...]
+
+
+def blocks_of(place_ref, a8, ay, b8, bx):
+    outer_me = place_ref[2] * 2 + place_ref[1]
     for j in range(16):
         rel_z, rel_y, rel_x = j >> 2, (j >> 1) & 1, j & 1
-        outer, xx = rel_places(me, rel_z, rel_y, rel_x)
         src_a = (ay if rel_y else a8).at[rel_x, rel_z]
         src_b = (bx if rel_x else b8).at[rel_y, rel_z]
+        yield j, outer_me ^ (rel_z * 2 + rel_y), place_ref[0] ^ rel_x, src_a, src_b
+
+
+def assemble_q_kernel(place_ref, a8, ay, b8, bx, out, vec_ref, up_ref, sems, lin_ref):
+    copies = []
+    for j, outer, xx, src_a, src_b in blocks_of(place_ref, a8, ay, b8, bx):
         copies.append(pltpu.make_async_copy(src_a, out.at[outer, 0, xx], sems.at[2 * j]))
         copies.append(pltpu.make_async_copy(src_b, out.at[outer, 1, xx], sems.at[2 * j + 1]))
     copy_all(copies)
-
-
-def assemble_down_kernel(me_ref, a8, ay, b8, bx, down, dense, sems):
-    me = me_ref[0]
+    lin_ref[...] = jnp.zeros_like(lin_ref)
+    lane = lax.broadcasted_iota(jnp.int32, (8, 128), 1)
+    for r in range(32):
+        block = out[r >> 2, (r >> 1) & 1, r & 1, 0:8, 3 * HALF : 3 * HALF + 128].astype(F32)
+        base, shift = divmod(288 * r, 128)
+        if shift:
+            block = pltpu.roll(block, shift, 1)
+        for k in range(3):
+            line = block[k : k + 1, :]
+            upper = lane[0:1, :] >= shift
+            lin_ref[base + k : base + k + 1, :] += jnp.where(upper, line, 0.0)
+            if shift:
+                lin_ref[base + k + 1 : base + k + 2, :] += jnp.where(upper, 0.0, line)
+    vec_ref[...] = jnp.zeros_like(vec_ref)
+    for u in range(6):
+        vec_ref[0:12, 128 * u : 128 * u + 128] = lin_ref[pl.ds(u, 12, stride=6), :]
+    is_zero = place_ref[3] == 0
+    tiles = [lin_ref[18 + t : 19 + t, :] for t in range(24)]
+    zero, one = half_tiles(tiles, 0), half_tiles(tiles, 1)
+    up_ref[...] = jnp.zeros_like(up_ref)
+    for t in range(12):
+        up_ref[0:1, 128 * t : 128 * t + 128] = jnp.where(is_zero, zero[t], one[t])
+
+
+def assemble_ud_kernel(place_ref, a8, ay, b8, bx, up, down, dense, sems):
     copies = []
-    for j in range(16):
-        rel_z, rel_y, rel_x = j >> 2, (j >> 1) & 1, j & 1
-        outer, xx = rel_places(me, rel_z, rel_y, rel_x)
-        src_a = (ay if rel_y else a8).at[rel_x, rel_z]
-        src_b = (bx if rel_x else b8).at[rel_y, rel_z]
-        copies.append(pltpu.make_async_copy(src_a, down.at[outer, xx, pl.ds(0, 64)], sems.at[j]))
+    for j, outer, xx, src_a, src_b in blocks_of(place_ref, a8, ay, b8, bx):
+        for c in range(2):
+            for h in range(2):
+                copies.append(
+                    pltpu.make_async_copy(
+                        src_a.at[pl.ds(24 * (2 * c + h), 24)],
+                        up.at[outer, c, xx, :, pl.ds(768 * h, 768)],
+                        sems.at[6 * j + 2 * c + h],
+                    )
+                )
         copies.append(
-            pltpu.make_async_copy(
-                src_b.at[pl.ds(0, 32)], down.at[outer, xx, pl.ds(64, 32)], sems.at[16 + j]
-            )
+            pltpu.make_async_copy(src_b.at[pl.ds(0, 96)], down.at[outer, xx], sems.at[6 * j + 4])
         )
         copies.append(
-            pltpu.make_async_copy(src_b.at[pl.ds(32, 24)], dense.at[outer, xx], sems.at[32 + j])
+            pltpu.make_async_copy(src_b.at[pl.ds(96, 24)], dense.at[outer, xx], sems.at[6 * j + 5])
         )
     copy_all(copies)
 
 
-def whole(shape):
-    return pl.BlockSpec(shape, lambda *_: (0,) * len(shape))
-
-
-def assemble(kernel, me, pieces, shapes, sem_count):
+def q_blocks(refs, part, outer, xx):
+    gq, gkv, lanes = refs
+    yield gq[outer, part, xx], slice(0, 24), slice(0, HALF)
+    yield gkv[outer, part, xx], slice(0, 24), slice(HALF, 3 * HALF)
+    yield lanes[outer, part, xx], slice(0, 24), slice(3 * HALF, Q_END)
+
+
+def ud_blocks(refs, part, outer, xx, core):
+    up, down, keep, got = refs
+    if part == 0:
+        for c in range(2):
+            for h in range(2):
+                at = 24 * (2 * c + h)
+                yield up[outer, c, xx, :, 768 * h : 768 * h + 768], slice(at, at + 24), slice(0, 768)
+    else:
+        yield down[outer, xx], slice(0, 96), slice(0, 768)
+        mine = lax.shift_right_logical(outer, 2) == core
+        for c in range(2):
+            value = jnp.where(mine, keep[outer & 3, c, xx], got[outer & 3, c, xx])
+            yield value, slice(96, 120), slice(HALF * c, HALF * c + HALF)
+
+
+def rs_first_kernel(blocks, count, place_ref, *refs):
+    x, y, core = place_ref[0], place_ref[1], place_ref[3]
+    ins, (send_a, send_b) = refs[:count], refs[count:]
+
+    def body(i, carry):
+        for value, rows, cols in blocks(ins, 0, i, 1 - x, core):
+            send_a[i, rows, cols] = value.astype(BF)
+        z, xx = lax.shift_right_logical(i, 1), i & 1
+        for value, rows, cols in blocks(ins, 1, 2 * z + 1 - y, xx, core):
+            send_b[i, rows, cols] = value.astype(BF)
+        return carry
+
+    lax.fori_loop(0, 8, body, 0)
+
+
+def rs_second_kernel(blocks, count, place_ref, *refs):
+    x, y, core = place_ref[0], place_ref[1], place_ref[3]
+    ins, (got_a, got_b, send_a, keep_a, send_b, keep_b) = refs[:count], refs[count:]
+
+    def body(z, carry):
+        for yy, out in ((1 - y, send_a), (y, keep_a)):
+            for value, rows, cols in blocks(ins, 0, 2 * z + yy, x, core):
+                total = value + got_a[2 * z + yy, rows, cols].astype(F32)
+                out[z, rows, cols] = total.astype(out.dtype)
+        for xx, out in ((1 - x, send_b), (x, keep_b)):
+            for value, rows, cols in blocks(ins, 1, 2 * z + y, xx, core):
+                total = value + got_b[2 * z + xx, rows, cols].astype(F32)
+                out[z, rows, cols] = total.astype(out.dtype)
+        return carry
+
+    lax.fori_loop(0, 4, body, 0)
+
+
+def rs_third_kernel(place_ref, keep_a, got_a, keep_b, got_b, s1, s2, s3, own):
+    z = place_ref[2]
+    cut = keep_a.shape[1]
+    for k, out in enumerate((own, s1, s2, s3)):
+        out[:cut] = (keep_a[z ^ k] + got_a[z ^ k].astype(F32)).astype(out.dtype)
+        out[cut:] = (keep_b[z ^ k] + got_b[z ^ k].astype(F32)).astype(out.dtype)
+
+
+def reduce_staged(blocks, place, inputs, shape_a, shape_b):
+    count = len(inputs)
+    dims = lambda n, shape: (n,) + shape
+    send_a, send_b = local_call(
+        functools.partial(rs_first_kernel, blocks, count), place, inputs,
+        [(dims(8, shape_a), BF), (dims(8, shape_b), BF)],
+    )
+    got = [swap(send_a, 1), swap(send_b, 4)]
+    send_a, keep_a, send_b, keep_b = local_call(
+        functools.partial(rs_second_kernel, blocks, count), place, inputs + got,
+        [(dims(4, s), k) for s in (shape_a, shape_b) for k in (BF, F32)],
+    )
+    got_a, got_b = swap(send_a, 4), swap(send_b, 1)
+    both = (shape_a[0] + shape_b[0], shape_a[1])
+    s1, s2, s3, own = local_call(
+        rs_third_kernel, place, [keep_a, got_a, keep_b, got_b],
+        [(both, BF)] * 3 + [(both, F32)],
+    )
+    return [own, swap(s1, 8), swap(s2, 16), swap(s3, 24)]
+
+
+def total_of(parts, rows, cols):
+    own, g1, g2, g3 = parts
+    return own[rows, cols] + g1[rows, cols].astype(F32) + g2[rows, cols].astype(F32) + g3[rows, cols].astype(F32)
+
+
+def end_q_kernel(place_ref, own, g1, g2, g3, keep, send):
+    core = place_ref[3]
+    parts = (own, g1, g2, g3)
+    keep[...] = total_of(parts, core, slice(None))
+    send[...] = total_of(parts, 1 - core, slice(None))
+
+
+def end_ud_kernel(place_ref, own, g1, g2, g3, keep, send, down):
+    is_zero = place_ref[3] == 0
+    parts = (own, g1, g2, g3)
+    every = slice(0, 768)
+    zero, one = total_of(parts, slice(0, 48), every), total_of(parts, slice(48, 96), every)
+    keep[0:48, :] = jnp.where(is_zero, zero, one)
+    send[0:48, :] = jnp.where(is_zero, one, zero)
+    down[...] = total_of(parts, slice(96, 192), every)
+    rest = total_of(parts, slice(192, 216), every)
+    blank = jnp.zeros((24, HALF), F32)
+    keep[48:72, 0:HALF] = jnp.where(is_zero, rest[:, :HALF], rest[:, HALF:])
+    send[48:72, 0:HALF] = jnp.where(is_zero, rest[:, HALF:], rest[:, :HALF])
+    keep[48:72, HALF:] = blank
+    send[48:72, HALF:] = blank
+
+
+def lanes_kernel(place_ref, sums, bdown, bup, norms, out, lin_ref):
+    is_zero = place_ref[3] == 0
+    zero128 = jnp.zeros((1, 128), F32)
+    for u in range(6):
+        at = slice(128 * (u % 3), 128 * (u % 3) + 128)
+        here = is_zero if u < 3 else jnp.logical_not(is_zero)
+        lin_ref[u : u + 1, :] = jnp.where(here, sums[0:1, at] + sums[8:9, at], zero128)
+        lin_ref[6 + u : 7 + u, :] = jnp.where(here, sums[1:2, at] + sums[9:10, at], zero128)
+        full = slice(128 * u, 128 * u + 128)
+        lin_ref[12 + u : 13 + u, :] = bdown[0:1, full]
+        lin_ref[42 + u : 43 + u, :] = bdown[0:1, full]
+        for k in range(4):
+            lin_ref[48 + 6 * k + u : 49 + 6 * k + u, :] = norms[k : k + 1, full]
+    tiles = [bup[0:1, 128 * t : 128 * t + 128] for t in range(12)]
+    none = [zero128] * 12
+    zero, one = full_tiles(tiles, none), full_tiles(none, tiles)
+    for t in range(24):
+        lin_ref[18 + t : 19 + t, :] = jnp.where(is_zero, zero[t], one[t])
+    lin_ref[72:80, :] = jnp.zeros((8, 128), F32)
+    out[...] = jnp.zeros_like(out)
+    lane = lax.broadcasted_iota(jnp.int32, (1, 128), 1)
+    for r in range(32):
+        base, shift = divmod(288 * r, 128)
+        for k in range(3):
+            line = lin_ref[base + k : base + k + 1, :]
+            if shift:
+                follow = lin_ref[base + k + 1 : base + k + 2, :]
+                back = 128 - shift
+                line = jnp.where(lane < back, pltpu.roll(line, back, 1), pltpu.roll(follow, back, 1))
+            if k == 2:
+                line = jnp.where(lane < 32, line, 0.0)
+            out[r >> 2, (r >> 1) & 1, r & 1, k : k + 1, :] = line
+
+
+def final_kernel(place_ref, q_keep, q_got, ud_keep, ud_got, down, grads, squares, rows_ref):
+    is_zero = place_ref[3] == 0
+    total = jnp.zeros((8, 128), F32)
+    for b in range(3):
+        span = slice(8 * b, 8 * b + 8)
+
+        def halves(keep, got, rows, cols):
+            k, g = keep[rows, cols], got[rows, cols]
+            return jnp.where(is_zero, k, g), jnp.where(is_zero, g, k)
+
+        def put(start, per, t, value):
+            rows_ref[pl.ds(start + 8 * per * b + t, 8, stride=per), :] = value
+            return value * value
+
+        for j in range(3):
+            for u in range(3):
+                at = slice(128 * (3 * j + u), 128 * (3 * j + u) + 128)
+                for c, value in enumerate(halves(q_keep, q_got, span, at)):
+                    total += put(0, 18, 6 * j + 3 * c + u, value)
+        for u in range(3):
+            at = slice(128 * u, 128 * u + 128)
+            for c, value in enumerate(halves(ud_keep, ud_got, slice(48 + 8 * b, 56 + 8 * b), at)):
+                total += put(AT_DENSE, 6, 3 * c + u, value)
+        pairs = [
+            halves(ud_keep, ud_got, slice(24 * (t // 6) + 8 * b, 24 * (t // 6) + 8 * b + 8), slice(128 * (t % 6), 128 * (t % 6) + 128))
+            for t in range(12)
+        ]
+        for t, value in enumerate(full_tiles([p[0] for p in pairs], [p[1] for p in pairs])):
+            total += put(AT_UP, 24, t, value)
+    for b in range(12):
+        for t in range(6):
+            value = down[8 * b : 8 * b + 8, 128 * t : 128 * t + 128]
+            rows_ref[pl.ds(AT_DOWN + 48 * b + t, 8, stride=6), :] = value
+            total += value * value
+    vec = q_keep[0:8, 3 * HALF : Q_END] + q_got[0:8, 3 * HALF : Q_END]
+    total += vec * vec
+    squares[...] = jnp.broadcast_to(jnp.sum(total, keepdims=True), (8, 128))
+    for k in range(AT_VEC // 8):
+        grads[0:1, 1024 * k : 1024 * k + 1024] = rows_ref[8 * k : 8 * k + 8, :].reshape(1, 1024)
+    base = AT_VEC * LANES
+    for k in range(2):
+        grads[0:1, base + 128 * k : base + 128 * k + 128] = vec[k : k + 1, :]
+    grads[0:1, base + 256 : base + 288] = vec[2:3, 0:32]
+
+
+def adam_kernel(squares, g_ref, p_ref, m_ref, v_ref, new_p, new_m, new_v):
+    updated = adam_update(p_ref[...], g_ref[...], m_ref[...], v_ref[...], squares[0:1, 0:1])
+    new_p[...], new_m[...], new_v[...] = updated
+
+
+def run_adam(squares, grads, params, first, second):
     return pl.pallas_call(
-        kernel,
-        out_shape=[jax.ShapeDtypeStruct(s, BF) for s in shapes],
-        in_specs=[pl.BlockSpec(memory_space=pltpu.SMEM)]
-        + [pl.BlockSpec(memory_space=pl.ANY)] * 4,
-        out_specs=[pl.BlockSpec(memory_space=pltpu.VMEM) for _ in shapes],
-        scratch_shapes=[pltpu.SemaphoreType.DMA((sem_count,))],
-        cost_estimate=pl.CostEstimate(flops=0, bytes_accessed=5_000_000, transcendentals=0),
-    )(me.reshape(1), *pieces)
+        adam_kernel,
+        in_specs=[VMEM] * 5,
+        out_specs=[VMEM] * 3,
+        out_shape=[jax.ShapeDtypeStruct(params.shape, F32)] * 3,
+        cost_estimate=pl.CostEstimate(flops=0, bytes_accessed=6_000_000, transcendentals=0),
+    )(squares, grads, params, first, second)
 
 
 def rope_chunk(u, cosine, low, high):
@@ -121,9 +445,9 @@
 
 def qkv_kernel(x_ref, w_ref, vec_ref, bias_ref, c_ref, lo_ref, hi_ref, q_ref, k_ref, v_ref, a1_ref, a2_ref):
     normed, _ = norm_rows(x_ref)
-    a1 = (normed * vec_ref[0:1, :] + vec_ref[1:2, :]).astype(BF)
+    a1 = (normed * vec_ref[8:9, :] + vec_ref[9:10, :]).astype(BF)
     a1_ref[...] = a1
-    a2_ref[...] = (normed * vec_ref[2:3, :] + vec_ref[3:4, :]).astype(BF)
+    a2_ref[...] = (normed * vec_ref[10:11, :] + vec_ref[11:12, :]).astype(BF)
     proj = jnp.dot(a1, w_ref[:, : 3 * HALF], preferred_element_type=F32)
     cosine, low, high = c_ref[...], lo_ref[...], hi_ref[...]
     for j in range(3):
@@ -139,7 +463,7 @@
     @pl.when(used_ref[0] > 0)
     def _():
         normed, _ = norm_rows(x_ref)
-        a1 = (normed * vec_ref[0:1, :] + vec_ref[1:2, :]).astype(BF)
+        a1 = (normed * vec_ref[8:9, :] + vec_ref[9:10, :]).astype(BF)
         a1_ref[...] = a1
         proj = jnp.dot(a1, w_ref[:, HALF : 3 * HALF], preferred_element_type=F32)
         cosine, low, high = c_ref[...], lo_ref[...], hi_ref[...]
@@ -413,102 +737,47 @@
     return pieces
 
 
-def core_parts(qkv, dense):
-    parts = []
-    for c in range(2):
-        cols = [qkv[:, D * j + HALF * c : D * j + HALF * c + HALF] for j in range(3)]
-        parts.append((jnp.concatenate(cols, axis=1), dense[:, HALF * c : HALF * c + HALF]))
-    return parts
-
-
-def up_halves(up, group):
-    rows = up.shape[0]
-    four = up.reshape(rows, FF // (2 * group), 2, group)
-    return four[:, :, 0].reshape(rows, FFH), four[:, :, 1].reshape(rows, FFH)
-
-
-def gather_staged(me, core, qkv, dense, up, down, vector):
-    group = 2 * down.shape[0]
-    rows = qkv.shape[0]
-    ups = up_halves(up, group)
-    halves = core_parts(qkv, dense)
-    lanes = jnp.pad(vector, (0, 384 - vector.shape[0])).reshape(3, 128)
-    lanes = jnp.pad(lanes, ((0, rows - 3), (0, 0)))
-    packed = [
-        jnp.concatenate([halves[c][0], lanes, ups[c], halves[c][1]], axis=1) for c in range(2)
-    ]
-    is_zero = core == 0
-    mine = jnp.where(is_zero, packed[0], packed[1])
-    other = swap(jnp.where(is_zero, packed[1], packed[0]), 2)
-    pair = jnp.where(is_zero, jnp.stack([mine, other]), jnp.stack([other, mine]))
-    q_end, u_end = 3 * HALF + 128, 3 * HALF + 128 + FFH
-    q_pieces = gather_pair(pair[:, :, :q_end], 1)
-    u_pieces = gather_pair(pair[:, :, q_end:u_end], 1)
-    dense_rows = jnp.concatenate([pair[0, :, u_end:], pair[1, :, u_end:]], axis=1)
-    d_pieces = gather_pair(jnp.concatenate([down, dense_rows], axis=0), 64)
-    return q_pieces, u_pieces, d_pieces
-
-
-def finish_vector(w_q):
-    lanes = w_q[:, :, :, :3, 3 * HALF :].reshape(32, 384)
-    return lanes[:, : NVEC // 32].reshape(NVEC)
-
-
-def split_vector(vector):
-    pieces, offset = [], 0
-    for extent in [D, D, D, FF, D, D, D, D, D]:
-        pieces.append(vector[offset : offset + extent].astype(F32))
-        offset += extent
-    return pieces
-
-
-def scatter_pair(part_a, part_b, place):
-    z, y, x = place
-    send_a = pick(part_a, 1 - x, 2).astype(BF)
-    send_b = pick(part_b, 1 - y, 2).astype(BF)
-    got_a, got_b = swap(send_a, 1), swap(send_b, 4)
-    sum_a = pick(part_a, x, 2) + got_a.astype(F32)
-    sum_b = pick(part_b, y, 2) + got_b.astype(F32)
-    got_a = swap(pick(sum_a, 1 - y, 1).astype(BF), 4)
-    got_b = swap(pick(sum_b, 1 - x, 1).astype(BF), 1)
-    sum_a = pick(sum_a, y, 1) + got_a.astype(F32)
-    sum_b = pick(sum_b, x, 1) + got_b.astype(F32)
-    both = jnp.concatenate([sum_a, sum_b], axis=1)
-    total = pick(both, z, 0)
-    for k in (1, 2, 3):
-        total = total + swap(pick(both, z ^ k, 0).astype(BF), 8 * k).astype(F32)
-    return total
-
-
 def on_device(tokens, out_grad, segments, positions, params, first_moment, second_moment):
     owners = lax.axis_size("dp") * lax.axis_size("ctx")
     staged = owners == 32
     me = (lax.axis_index("dp") * lax.axis_size("ctx") + lax.axis_index("ctx")).astype(jnp.int32)
     ctx, core = me & 1, (me >> 1) & 1
+    place = jnp.stack([ctx, (me >> 2) & 1, me >> 3, core])
     is_zero = core == 0
     rows = tokens.shape[0]
-    flat = params.reshape(-1)
-    qkv, dense, up, down, vector = split_shard(flat.astype(BF), owners)
-    group = 2 * down.shape[0]
-
-    far_own = lax.ppermute(tokens, AX, [(i, i + 1) for i in range(0, owners, 2)])
-    tokens_other = swap(tokens, 2)
-    grad_other = swap(out_grad, 2)
-    positions_all = jnp.concatenate([positions, swap(positions, 2)])
+    group = 2 * (FF // owners)
 
     if staged:
-        q_pieces, u_pieces, d_pieces = gather_staged(me, core, qkv, dense, up, down, vector)
-        w_q5 = assemble(assemble_pair_kernel, me, [p.reshape(p.shape[:2] + p.shape[-2:]) for p in q_pieces],
-                        [(8, 2, 2, D // 32, 3 * HALF + 128)], 32)[0]
-        w_u5 = assemble(assemble_pair_kernel, me, [p.reshape(p.shape[:2] + p.shape[-2:]) for p in u_pieces],
-                        [(8, 2, 2, D // 32, FFH)], 32)[0]
-        w_d4, dense5 = assemble(assemble_down_kernel, me, d_pieces,
-                                [(8, 2, FF // 32, D), (8, 2, D // 32, D)], 48)
-        vector = finish_vector(w_q5)
-        w_q = w_q5.reshape(D, 3 * HALF + 128)
+        mine, other, own_rows = local_call(
+            prep_kernel, place, [params],
+            [((24, PACK), BF), ((24, PACK), BF), ((96, D), BF)],
+            scratch=[pltpu.VMEM((AT_END, LANES), F32)],
+        )
+        got = swap(other, 2)
+        q_pair = local_call(regroup_q_kernel, place, [mine, got], [((2, 24, Q_END), BF)])[0]
+        q_pieces, after = gather_pair(q_pair, 1)
+        ud_block = local_call(
+            regroup_ud_kernel, place, [mine, got, own_rows, after], [((216, D), BF)],
+            in_specs=[VMEM] * 3 + [HBM],
+        )[0]
+        ud_pieces, _ = gather_pair(ud_block, ROWS_A)
+        w_q5, vecs, bias_up_half = local_call(
+            assemble_q_kernel, place, [p.reshape(p.shape[:2] + p.shape[-2:]) for p in q_pieces],
+            [((8, 2, 2, 24, Q_END), BF), ((16, D), F32), ((8, FFH), F32)],
+            scratch=[pltpu.SemaphoreType.DMA((32,)), pltpu.VMEM((80, 128), F32)],
+            in_specs=[HBM] * 4,
+        )
+        bias_up_half = bias_up_half[0]
+        w_u5, w_d4, dense5 = local_call(
+            assemble_ud_kernel, place, list(ud_pieces),
+            [((8, 2, 2, 24, FFH), BF), ((8, 2, 96, D), BF), ((8, 2, 24, D), BF)],
+            scratch=[pltpu.SemaphoreType.DMA((96,))],
+            in_specs=[HBM] * 4,
+        )
+        w_q = w_q5.reshape(D, Q_END)
         w_up = w_u5.reshape(D, FFH)
         w_down = w_d4.reshape(FFH, D)
-        dense_mine = dense5.reshape(8, 2, D // 32, 2, HALF).transpose(0, 3, 1, 2, 4).reshape(D, HALF)
+        dense_mine = dense5.reshape(8, 2, 24, 2, HALF).transpose(0, 3, 1, 2, 4).reshape(D, HALF)
         dense_got = swap(dense_mine, 2)
         w_dense = jnp.where(
             is_zero,
@@ -516,21 +785,23 @@
             jnp.concatenate([dense_got, dense_mine], axis=1),
         )
     else:
-        full = [lax.all_gather(p, AX, axis=0, tiled=True) for p in (qkv, dense, up, down, vector)]
+        shards = split_shard(params.reshape(-1).astype(BF), owners)
+        full = [lax.all_gather(p, AX, axis=0, tiled=True) for p in shards]
         w_q = pick(full[0].reshape(D, 3, 2, HALF), core, 2).reshape(D, 3 * HALF)
         w_dense = full[1]
         w_up = pick(full[2].reshape(D, FFH // group, 2, group), core, 2).reshape(D, FFH)
         w_down = pick(full[3].reshape(FFH // group, 2, group, D), core, 1).reshape(FFH, D)
-        vector = full[4]
-    bias_q, bias_v, bias_dense, bias_up, bias_down, gain_one, shift_one, gain_two, shift_two = (
-        split_vector(vector)
-    )
+        vecs = jnp.pad(full[4].astype(F32).reshape(12, D), ((0, 4), (0, 0)))
+        bias_up_half = pick(vecs[3:7].reshape(FFH // group, 2, group), core, 1).reshape(FFH)
     half_of = lambda v: jnp.where(is_zero, v[:HALF], v[HALF:])
-    bias_up_half = pick(bias_up.reshape(FFH // group, 2, group), core, 1).reshape(FFH)
     dense_rows = lax.dynamic_slice_in_dim(w_dense, core * HALF, HALF, 0)
-    vecs = jnp.stack([gain_one, shift_one, gain_two, shift_two] + [jnp.zeros_like(gain_one)] * 4)
-    biases = jnp.stack([half_of(bias_q), half_of(bias_v)] + [jnp.zeros((HALF,), F32)] * 6)
-
+    biases = jnp.stack([half_of(vecs[0]), half_of(vecs[1])] + [jnp.zeros((HALF,), F32)] * 6)
+    gain_one, gain_two = vecs[8], vecs[10]
+
+    far_own = lax.ppermute(tokens, AX, [(i, i + 1) for i in range(0, owners, 2)])
+    tokens_other = swap(tokens, 2)
+    grad_other = swap(out_grad, 2)
+    positions_all = jnp.concatenate([positions, swap(positions, 2)])
     x_all = jnp.concatenate([tokens, tokens_other], axis=0)
     g_all = jnp.concatenate([out_grad, grad_other], axis=0)
     x_far = jnp.concatenate([far_own, swap(far_own, 2)], axis=0)
@@ -541,7 +812,6 @@
     tables = rotary_tables(positions_all)
     tables_far = rotary_tables(far_positions)
     least = jnp.min(start.reshape(-1, QB), axis=1)
-    blocks = rows // QB
     plan = jnp.where(least < 0, -((QB - 1 - least) // QB), least // QB)
     used = ctx.reshape(1)
 
@@ -552,11 +822,31 @@
     pre = jnp.dot(a2, w_up, preferred_element_type=F32) + bias_up_half
     act = gelu_exact(pre).astype(BF)
     grad_down = jnp.dot(act.T, g_all, preferred_element_type=F32)
-    grad_dense = jnp.dot(att.T, g_all, preferred_element_type=F32)
     grad_pre = jnp.dot(g_all, w_down.T, preferred_element_type=F32) * gelu_slope(pre)
     grad_pre_low = grad_pre.astype(BF)
     grad_bias_up = jnp.sum(grad_pre, axis=0)
     grad_up = jnp.dot(a2.T, grad_pre_low, preferred_element_type=F32)
+    g_keep = jnp.where(is_zero, g_all[:, :HALF], g_all[:, HALF:])
+    g_send = jnp.where(is_zero, g_all[:, HALF:], g_all[:, :HALF])
+    dense_keep = jnp.dot(att.T, g_keep, preferred_element_type=F32)
+    dense_send = jnp.dot(att.T, g_send, preferred_element_type=F32)
+
+    if staged:
+        quarter = (4, 2, 2, 24, HALF)
+        ud_sums = reduce_staged(
+            ud_blocks, place,
+            [
+                grad_up.reshape(8, 2, 2, 24, FFH),
+                grad_down.reshape(8, 2, 96, D),
+                dense_keep.reshape(quarter),
+                swap(dense_send, 2).reshape(quarter),
+            ],
+            (ROWS_A, D), (216 - ROWS_A, D),
+        )
+        ud_keep, ud_send, own_down = local_call(
+            end_ud_kernel, place, ud_sums, [((72, D), F32), ((72, D), F32), ((96, D), F32)]
+        )
+        ud_got = swap(ud_send, 2)
 
     grad_att = jnp.dot(g_all, dense_rows.T, preferred_element_type=F32).astype(BF)
     gq, gk, gv, gkf, gvf, sums = attn_bwd(
@@ -568,7 +858,6 @@
     grad_kv_cols = jnp.dot(a1.T, gkv, preferred_element_type=F32) + jnp.dot(
         a1f.T, gkvf, preferred_element_type=F32
     )
-    grad_qkv = jnp.concatenate([grad_q_cols, grad_kv_cols], axis=1)
 
     normed, inverse = normalize(x_all.astype(F32))
     normed_far, _ = normalize(x_far.astype(F32))
@@ -578,113 +867,80 @@
     )
     ga1f = jnp.dot(gkvf, w_qkv[:, HALF:].T, preferred_element_type=F32)
     ga2 = jnp.dot(grad_pre_low, w_up.T, preferred_element_type=F32)
-    grad_gain_one = jnp.sum(ga1 * normed, axis=0) + jnp.sum(ga1f * normed_far, axis=0)
-    grad_shift_one = jnp.sum(ga1, axis=0) + jnp.sum(ga1f, axis=0)
-    grad_gain_two = jnp.sum(ga2 * normed, axis=0)
-    grad_shift_two = jnp.sum(ga2, axis=0)
-
+    norm_grads = [
+        jnp.sum(ga1 * normed, axis=0) + jnp.sum(ga1f * normed_far, axis=0),
+        jnp.sum(ga1, axis=0) + jnp.sum(ga1f, axis=0),
+        jnp.sum(ga2 * normed, axis=0),
+        jnp.sum(ga2, axis=0),
+    ]
     cotangent = out_grad.astype(F32)
     grad_bias_out = jnp.sum(cotangent, axis=0)
-    sums = jnp.sum(sums.reshape(2, 8, HALF), axis=0)
-    nothing = jnp.zeros((HALF,), F32)
-    spread = lambda v: jnp.where(
-        is_zero, jnp.concatenate([v, nothing]), jnp.concatenate([nothing, v])
-    )
-    up_groups = grad_bias_up.reshape(FFH // group, group)
-    up_zero = jnp.zeros_like(up_groups)
-    grad_bias_up_full = jnp.where(
-        is_zero,
-        jnp.stack([up_groups, up_zero], axis=1),
-        jnp.stack([up_zero, up_groups], axis=1),
-    ).reshape(FF)
-    grad_vector = jnp.concatenate(
-        [
-            spread(sums[0]),
-            spread(sums[1]),
-            grad_bias_out,
-            grad_bias_up_full,
-            grad_bias_out,
-            grad_gain_one,
-            grad_shift_one,
-            grad_gain_two,
-            grad_shift_two,
-        ]
-    )
 
     if staged:
-        per = D // 32
-        z, y, x = me >> 3, (me >> 2) & 1, ctx
-        place = (z, y, x)
-        dense_cols = [grad_dense[:, :HALF], grad_dense[:, HALF:]]
-        keep = jnp.where(is_zero, dense_cols[0], dense_cols[1])
-        got = swap(jnp.where(is_zero, dense_cols[1], dense_cols[0]), 2)
-        dense_half = jnp.where(
-            is_zero,
-            jnp.concatenate([keep, got], axis=0),
-            jnp.concatenate([got, keep], axis=0),
-        )
-        d6 = dense_half.reshape(4, 2, 2, 2, per, HALF)
-        dn = grad_down.reshape(4, 2, 2, FF // 32, D)
-        dense_wide = jnp.concatenate([d6[:, :, 0], d6[:, :, 1]], axis=-1)
-        part_b = jnp.concatenate([dn[:, :, :, 64:], dense_wide], axis=3)
-        done_d = scatter_pair(dn[:, :, :, :64], part_b.transpose(0, 2, 1, 3, 4), place)
-        up6 = grad_up.reshape(4, 2, 2, 2, per, FFH)
-        done_u = scatter_pair(up6[:, :, 0], up6[:, :, 1].transpose(0, 2, 1, 3, 4), place)
-        lanes = jnp.pad(grad_vector.reshape(32, NVEC // 32), ((0, 0), (0, 384 - NVEC // 32)))
-        lanes = jnp.pad(lanes.reshape(32, 3, 128), ((0, 0), (0, per - 3), (0, 0)))
-        grad_q = jnp.concatenate([grad_qkv, lanes.reshape(D, 128)], axis=1)
-        q6 = grad_q.reshape(4, 2, 2, 2, per, 3 * HALF + 128)
-        done_q = scatter_pair(q6[:, :, 0], q6[:, :, 1].transpose(0, 2, 1, 3, 4), place)
-
-        def core_swap(first, second):
-            kept = jnp.where(is_zero, first, second)
-            return kept, swap(jnp.where(is_zero, second, first), 2)
-
-        def in_order(kept, got, axis):
-            return jnp.where(
-                is_zero,
-                jnp.concatenate([kept, got], axis=axis),
-                jnp.concatenate([got, kept], axis=axis),
-            )
-
-        q_keep, q_got = core_swap(done_q[:per], done_q[per:])
-        u_keep, u_got = core_swap(done_u[:per], done_u[per:])
-        e_keep, e_got = core_swap(
-            done_d[FF // 32 :, :HALF], done_d[FF // 32 :, HALF:]
-        )
-        own_qkv = jnp.concatenate(
+        lanes = local_call(
+            lanes_kernel, place,
+            [sums, grad_bias_out[None], grad_bias_up[None], jnp.stack(norm_grads)],
+            [((8, 2, 2, 24, 128), F32)],
+            scratch=[pltpu.VMEM((80, 128), F32)],
+        )[0]
+        q_sums = reduce_staged(
+            lambda refs, part, outer, xx, _: q_blocks(refs, part, outer, xx), place,
             [
-                in_order(q_keep[:, HALF * j : HALF * j + HALF], q_got[:, HALF * j : HALF * j + HALF], 1)
-                for j in range(3)
+                grad_q_cols.reshape(8, 2, 2, 24, HALF),
+                grad_kv_cols.reshape(8, 2, 2, 24, D),
+                lanes,
             ],
-            axis=1,
-        )
-        own_vec = (q_keep[:3, 3 * HALF :] + q_got[:3, 3 * HALF :]).reshape(384)[: NVEC // 32]
-        own_dense = in_order(e_keep, e_got, 1)
-        three = lambda t: t.reshape(per, FFH // group, 1, group)
-        own_up = in_order(three(u_keep), three(u_got), 2).reshape(per, FF)
-        own_down = done_d[: FF // 32]
+            (24, Q_END), (24, Q_END),
+        )
+        q_sums = [t.reshape(2, 24, Q_END) for t in q_sums]
+        q_keep, q_send = local_call(end_q_kernel, place, q_sums, [((24, Q_END), F32)] * 2)
+        grads, squares = local_call(
+            final_kernel, place, [q_keep, swap(q_send, 2), ud_keep, ud_got, own_down],
+            [((1, NPAR), F32), ((8, 128), F32)],
+            scratch=[pltpu.VMEM((AT_END, LANES), F32)],
+        )
     else:
+        sums = jnp.sum(sums.reshape(2, 8, HALF), axis=0)
+        nothing = jnp.zeros((HALF,), F32)
+        spread = lambda t: jnp.where(
+            is_zero, jnp.concatenate([t, nothing]), jnp.concatenate([nothing, t])
+        )
         widen = lambda t, axis: lax.dynamic_update_slice_in_dim(
             jnp.zeros(t.shape[:axis] + (2,) + t.shape[axis + 1 :], F32), t, core, axis
         )
+        grad_vector = jnp.concatenate(
+            [
+                spread(sums[0]),
+                spread(sums[1]),
+                grad_bias_out,
+                widen(grad_bias_up.reshape(FFH // group, 1, group), 1).reshape(FF),
+                grad_bias_out,
+                *norm_grads,
+            ]
+        )
         scatter = lambda t: lax.psum_scatter(t, AX, scatter_dimension=0, tiled=True)
-        own_qkv = scatter(widen(grad_qkv.reshape(D, 3, 1, HALF), 2).reshape(D, 3 * D))
-        own_dense = scatter(widen(grad_dense.reshape(1, HALF, D), 0).reshape(D, D))
-        own_up = scatter(widen(grad_up.reshape(D, FFH // group, 1, group), 2).reshape(D, FF))
-        own_down = scatter(widen(grad_down.reshape(FFH // group, 1, group, D), 1).reshape(FF, D))
-        own_vec = scatter(grad_vector)
-
-    grads = jnp.concatenate(
-        [own_qkv.reshape(-1), own_dense.reshape(-1), own_up.reshape(-1), own_down.reshape(-1), own_vec]
-    )
-    squares = jnp.broadcast_to(jnp.sum(grads * grads), (8, 128))
+        grad_qkv = jnp.concatenate([grad_q_cols, grad_kv_cols], axis=1)
+        dense_both = jnp.where(
+            is_zero,
+            jnp.concatenate([dense_keep, dense_send], axis=1),
+            jnp.concatenate([dense_send, dense_keep], axis=1),
+        )
+        pieces = [
+            scatter(widen(grad_qkv.reshape(D, 3, 1, HALF), 2).reshape(D, 3 * D)),
+            scatter(widen(dense_both.reshape(1, HALF, D), 0).reshape(D, D)),
+            scatter(widen(grad_up.reshape(D, FFH // group, 1, group), 2).reshape(D, FF)),
+            scatter(widen(grad_down.reshape(FFH // group, 1, group, D), 1).reshape(FF, D)),
+            scatter(grad_vector),
+        ]
+        grads = jnp.concatenate([t.reshape(1, -1) for t in pieces], axis=1)
+        squares = jnp.broadcast_to(jnp.sum(grads * grads), (8, 128))
+
     bit = 1
     while bit < owners:
         squares = squares + swap(squares, bit)
         bit *= 2
-    new_params, new_first, new_second = adam_update(
-        flat, grads, first_moment.reshape(-1), second_moment.reshape(-1), squares[0, 0]
+    new_params, new_first, new_second = run_adam(
+        squares, grads, params, first_moment, second_moment
     )
 
     partial_result = jnp.dot(att, dense_rows, preferred_element_type=F32) + jnp.dot(
@@ -694,7 +950,7 @@
         tokens.astype(F32)
         + partial_result[:rows]
         + swap(partial_result[rows:], 2)
-        + (bias_dense + bias_down)
+        + (vecs[2] + vecs[7])
     ).astype(BF)
     gx = ga1 * gain_one + ga2 * gain_two
     gx_far = ga1f * gain_one
@@ -707,8 +963,7 @@
         - jnp.mean(grad_normed, axis=1, keepdims=True)
         - own_normed * jnp.mean(grad_normed * own_normed, axis=1, keepdims=True)
     )
-    row = lambda t: t.reshape(1, -1)
-    return (result, grad_inputs, row(grads), row(new_params), row(new_first), row(new_second))
+    return (result, grad_inputs, grads, new_params, new_first, new_second)
 
 
 def solution(mesh):

time: 440 us -> 374 us (0.85)
  local copies, waits for them, and re-layouts: 73 us -> 26 us
  Pallas kernels: 56.9 us -> 102 us
  other arithmetic: 67.9 us -> 35.8 us
  starting transfers between devices: 91.5 us -> 67.4 us
  waiting for transfers between devices: 91.8 us -> 85.4 us
    pallas_call x3 -> x16, Pallas kernels: 10.4 us -> 54.6 us  [the longest x15 50.2 us: local_call(): pl.pallas_call(kernel, out_shape=[jax.ShapeDtypeStruct(shape, kind) for s...]
    ppermute x60 -> x45, starting transfers between devices: 85.7 us -> 62.7 us  [swap(): return lax.ppermute(value, AX, [(i, i ^ mask) for i in range(size)])]
    reshape x14 -> x1, local copies, waits for them, and re-layouts: 15.6 us -> 0.06 us  [on_device(): dense5.reshape(8, 2, 24, 2, HALF).transpose(0, 3, 1, 2, 4).reshape(D, HALF)]
    unnamed x170 -> x105, local copies, waits for them, and re-layouts: 26.6 us -> 14.2 us
    ppermute x1, waiting for transfers between devices: 9.88 us -> 0.01 us  [on_device(): lax.ppermute(tokens, AX, [(i, i + 1) for i in range(0, owners, 2)])]
    add x16 -> x2, other arithmetic: 7.95 us -> 0.01 us  [the longest x1 0.01 us: on_device(): jnp.sum(ga1 * normed, axis=0) + jnp.sum(ga1f * normed_far, axis=0)]
    select_n x14 -> x0, other arithmetic: 7.81 us -> none  [the longest x5 2.82 us: in_order(): jnp.where(is_zero, jnp.concatenate([kept, got], axis=axis), jnp.concatena...]
    sub x1 -> x0, other arithmetic: 7.47 us -> none  [adam_update(): params - learn_rate * (corrected_first / (jnp.sqrt(corrected_second) + ad...]
  transfers between devices with their start and end apart: 62 -> 47, of which waited for: 21 -> 17; matrix products, arithmetic and copies ran while one was open for 38% -> 28% of each run, Pallas kernels for 13% -> 26%
where the time goes in v2:
time: 374 us; the launch traced here: 369 us
  Pallas kernels  102 us (27%)
  waiting for transfers between devices  85.4 us (23%)
  starting transfers between devices  67.4 us (18%)
  matrix products  51 us (14%)
  other arithmetic  35.8 us (10%)
  local copies, waits for them, and re-layouts  26 us (7%)
    ppermute x45, waiting for transfers between devices, swap(): return lax.ppermute(value, AX, [(i, i ^ mask) for i in range(size)])  79.9 us
    ppermute x45, starting transfers between devices, swap(): return lax.ppermute(value, AX, [(i, i ^ mask) for i in range(size)])  62.7 us
    pallas_call x15, Pallas kernels, local_call(): pl.pallas_call(kernel, out_shape=[jax.ShapeDtypeStruct(shape, kind) for s...  50.2 us
    pallas_call x1, Pallas kernels, attn_bwd(): pl.pallas_call(functools.partial(attn_bwd_kernel, rows), grid_spec=pltpu....  19.2 us
    pallas_call x1, Pallas kernels, attn_fwd(): pl.pallas_call(functools.partial(attn_fwd_kernel, rows), grid_spec=pltpu....  14.9 us
    unnamed x105, local copies, waits for them, and re-layouts  14.2 us
    pallas_call x1, Pallas kernels, run_qkv(): pl.pallas_call(qkv_kernel, grid=(rows // blk,), in_specs=specs, out_specs...  7.75 us
  transfers between devices with their start and end apart: 47, of which 17 were waited for; matrix products, arithmetic and copies ran while one was open for 28% of the time, Pallas kernels for 26%

profile of v2, /device:TPU:0, one launch (start us, length us, event | category | flops | bytes accessed | tf_op | source)
XLA Modules:
  0.0 369.0 jit_solution(14342152075629693790)
XLA Ops:
  7.3 5.1 %bitcast_select_fusion = f32[128]{0:T(128)S(1)} fusion(f32[]{:T(128)} %bitcast.19, f32[]{:T(128)} %bitcast.20, f32[]{:T(128)} %bitcast.21, f32[]{:T(128)} %bitcast.22, f32[]{:T(128)} %bitcast.23, f32[]{:T(128)} %bitcast.25, f32[]{:T(128)} %bitcast.24, f32[]{:T(128)} %bitcast.18), kind=kLoop, calls=%fused_computation.119 | loop fusion | flops 4352 | bytes 544 | tf_op jit(solution)/shard_map/gather | solution.py:692
  16.3 4.6 %collective-permute-start.5 = (bf16[2,24,1280]{2,1,0:T(8,128)(2,1)}, bf16[2,24,1280]{2,1,0:T(8,128)(2,1)S(1)}, u32[]{:S(2)}, u32[]{:S(2)}) collective-permute-start(bf16[2,24,1280]{2,1,0:T(8,128)(2,1)} %shard_map.110), channel_id=1, source_target_pairs={{0,24},{1,25},{2,26},{3,27},{4,28},{5,29},{6,30},{7,31},{8,16},{9,... | collective-permute-start | bytes 368648 | tf_op jit(solution)/shard_map/ppermute | solution.py:35
  21.4 5.6 %fusion.32 = (f32[1024,128]{1,0:T(8,128)}, f32[1024,128]{1,0:T(8,128)}, f32[1024,128]{1,0:T(8,128)}, f32[1024,128]{1,0:T(8,128)}, f32[1024,128]{1,0:T(8,128)}, /*index=5*/f32[1024,128]{1,0:T(8,128)}) fusion(f32[128]{0:T(128)S(1)} %bitcast_select_fusion, f32[1024]{0:T(1024)S(1)} %convert_element_type.48, pred[128]{0:T(512)(128)(4,1)S(1)} %get-tuple-element.166, ...), kind=kLoop, calls=%fused_computation.66 | loop fusion | flops 1310720 | bytes 3154816 | tf_op jit(solution)/shard_map/jit(_where)/select_n | solution.py:696
  27.2 4.9 %collective-permute-done.4 = bf16[2,24,1280]{2,1,0:T(8,128)(2,1)S(1)} collective-permute-done((bf16[2,24,1280]{2,1,0:T(8,128)(2,1)}, bf16[2,24,1280]{2,1,0:T(8,128)(2,1)S(1)}, u32[]{:S(2)}, u32[]{:S(2)}) %collective-permute-start.4) | collective-permute-done | bytes 122912 | tf_op jit(solution)/shard_map/ppermute | solution.py:35
  46.4 5.7 %collective-permute-done.14 = bf16[216,768]{1,0:T(8,128)(2,1)S(1)} collective-permute-done((bf16[216,768]{1,0:T(8,128)(2,1)}, bf16[216,768]{1,0:T(8,128)(2,1)S(1)}, u32[]{:S(2)}, u32[]{:S(2)}) %collective-permute-start.14) | collective-permute-done | bytes 331808 | tf_op jit(solution)/shard_map/ppermute | solution.py:35
  55.5 13.7 %collective-permute-done.13 = bf16[216,768]{1,0:T(8,128)(2,1)S(1)} collective-permute-done((bf16[216,768]{1,0:T(8,128)(2,1)}, bf16[216,768]{1,0:T(8,128)(2,1)S(1)}, u32[]{:S(2)}, u32[]{:S(2)}) %collective-permute-start.13) | collective-permute-done | bytes 331808 | tf_op jit(solution)/shard_map/ppermute | solution.py:35
  79.1 4.2 %collective-permute-done.9 = bf16[2,4,1,24,1280]{4,3,1,2,0:T(8,128)(2,1)S(1)} collective-permute-done((bf16[2,4,1,24,1280]{4,3,1,2,0:T(8,128)(2,1)S(1)}, bf16[2,4,1,24,1280]{4,3,1,2,0:T(8,128)(2,1)S(1)}, u32[]{:S(2)}, u32[]{:S(2)}) %collective-permute-start.9) | collective-permute-done | bytes 491552 | tf_op jit(solution)/shard_map/ppermute | solution.py:35
  84.9 3.9 %shard_map.111 = (bf16[8,2,2,24,1280]{4,3,2,1,0:T(8,128)(2,1)}, f32[16,768]{1,0:T(8,128)}, f32[8,1536]{1,0:T(8,128)}) custom-call(s32[4]{0:T(128)} %pad_add_fusion.place_ref, bf16[2,4,24,1280]{3,2,1,0:T(8,128)(2,1)} %get-tuple-element.142.a8, bf16[2,4,24,1280]{3,2,1,0:T(8,128)(2,1)} %bitcast.127, bf16[2,4,24,1280]{3,2,1,0:T(8,128)(2,1)} %get-tuple-element.136.b8, ...), custom_call_target="tpu_custom_call" | custom-call | bytes 4000000 | tf_op jit(solution)/shard_map/pallas_call | solution.py:61
  93.0 7.8 %shard_map.112 = (bf16[1024,384]{1,0:T(8,128)(2,1)}, bf16[1024,384]{1,0:T(8,128)(2,1)}, bf16[1024,384]{1,0:T(8,128)(2,1)}, bf16[1024,768]{1,0:T(8,128)(2,1)}, bf16[1024,768]{1,0:T(8,128)(2,1)}) custom-call(bf16[1024,768]{1,0:T(8,128)(2,1)} %copy-done, bf16[768,1280]{1,0:T(8,128)(2,1)} %bitcast.131, f32[16,768]{1,0:T(8,128)} %get-tuple-element.64.vec_ref, ...), custom_call_target="tpu_custom_call" | custom-call | flops 1811939328 | bytes 8000000 | tf_op jit(solution)/shard_map/pallas_call | solution.py:491
  108.5 5.0 %shard_map.113 = (bf16[1024,384]{1,0:T(8,128)(2,1)}, bf16[1024,384]{1,0:T(8,128)(2,1)}, bf16[1024,768]{1,0:T(8,128)(2,1)}) custom-call(s32[1]{0:T(128)} %bitcast.used_ref, bf16[1024,768]{1,0:T(8,128)(2,1)} %copy-done.4, bf16[768,1280]{1,0:T(8,128)(2,1)} %bitcast.132, f32[16,768]{1,0:T(8,128)} %get-tuple-element.64.vec_ref, ...), custom_call_target="tpu_custom_call" | custom-call | flops 1811939328 | bytes 8000000 | tf_op jit(solution)/shard_map/pallas_call | solution.py:499
  113.5 14.9 %shard_map.114 = (bf16[1024,384]{1,0:T(8,128)(2,1)}, f32[1024,384]{1,0:T(8,128)}) custom-call(s32[4]{0:T(128)} %fusion.50.plan_ref, bf16[1024,384]{1,0:T(8,128)(2,1)} %get-tuple-element.65.q_ref, bf16[1024,384]{1,0:T(8,128)(2,1)} %get-tuple-element.66.k_ref, bf16[1024,384]{1,0:T(8,128)(2,1)} %get-tuple-element.67.v_ref, ...), custom_call_target="tpu_custom_call" | custom-call | flops 20000000000 | bytes 6000000 | tf_op jit(solution)/shard_map/pallas_call | solution.py:647
  135.3 6.5 %shard_map.116 = (bf16[8,2,2,24,1536]{4,3,2,1,0:T(8,128)(2,1)}, bf16[8,2,96,768]{3,2,1,0:T(8,128)(2,1)}, bf16[8,2,24,768]{3,2,1,0:T(8,128)(2,1)}) custom-call(s32[4]{0:T(128)} %pad_add_fusion.place_ref, bf16[2,4,96,768]{3,2,1,0:T(8,128)(2,1)} %pad_maximum_fusion.1.a8, bf16[2,4,96,768]{3,2,1,0:T(8,128)(2,1)} %collective-permute-done.16.ay, ...), custom_call_target="tpu_custom_call" | custom-call | bytes 4000000 | tf_op jit(solution)/shard_map/pallas_call | solution.py:61
  141.8 5.3 %multiply_convert_fusion = (bf16[1024,1536]{1,0:T(8,128)(2,1)S(1)}, f32[1024,1536]{1,0:T(8,128)S(1)}) fusion(f32[1536]{0:T(1024)S(1)} %copy-done.41, bf16[1024,768]{1,0:T(8,128)(2,1)} %get-tuple-element.73, bf16[768,1536]{1,0:T(8,128)(2,1)} %bitcast.143), kind=kOutput, calls=%fused_computation.6 | convolution fusion | flops 2425356288 | bytes 13375488 | tf_op jit(solution)/shard_map/dot_general | solution.py:822
  147.1 5.6 %fusion.58 = (f32[1536]{0:T(1024)S(1)}, bf16[1024,1536]{1,0:T(8,128)(2,1)S(1)}) fusion(f32[1024,1536]{1,0:T(8,128)S(1)} %get-tuple-element.163, f32[1536]{0:T(1024)S(1)} %copy-done.41, bf16[1024,768]{1,0:T(8,128)(2,1)S(1)} %copy-done.32, bf16[1536,768]{1,0:T(8,128)(2,1)S(1)} %bitcast.142), kind=kOutput, calls=%fused_computation.155 | convolution fusion | flops 2434791936 | bytes 13381632 | tf_op jit(solution)/shard_map/dot_general | solution.py:825
  152.8 4.3 %fusion.20 = f32[1024,768]{1,0:T(8,128)} fusion(bf16[768,1536]{1,0:T(8,128)(2,1)S(1)} %bitcast.144, bf16[1024,1536]{1,0:T(8,128)(2,1)S(1)} %get-tuple-element.165), kind=kOutput, calls=%fused_computation.38 | convolution fusion | flops 2415919104 | bytes 8650752 | tf_op jit(solution)/shard_map/dot_general | solution.py:869
  157.1 4.4 %fusion.18 = f32[768,1536]{1,0:T(8,128)} fusion(bf16[1024,768]{1,0:T(8,128)(2,1)S(1)} %copy-done.16, bf16[1024,1536]{1,0:T(8,128)(2,1)S(1)} %get-tuple-element.165), kind=kOutput, calls=%fused_computation.36 | convolution fusion | flops 2415919104 | bytes 9437184 | tf_op jit(solution)/shard_map/dot_general | solution.py:828
  162.2 4.4 %fusion.62 = f32[1536,768]{1,0:T(8,128)} fusion(bf16[1024,1536]{1,0:T(8,128)(2,1)S(1)} %get-tuple-element.162, bf16[1024,768]{1,0:T(8,128)(2,1)S(1)} %copy-done.32), kind=kOutput, calls=%fused_computation.159 | convolution fusion | flops 2415919104 | bytes 9437184 | tf_op jit(solution)/shard_map/dot_general | solution.py:824
  166.6 5.9 %shard_map.123 = (bf16[8,96,768]{2,1,0:T(8,128)(2,1)}, bf16[8,120,768]{2,1,0:T(8,128)(2,1)}) custom-call(s32[4]{0:T(128)} %pad_add_fusion.place_ref, f32[8,2,2,24,1536]{4,3,2,1,0:T(8,128)} %bitcast.96, f32[8,2,96,768]{3,2,1,0:T(8,128)} %bitcast.98, f32[4,2,2,24,384]{4,3,2,1,0:T(8,128)} %bitcast.122, f32[4,2,2,24,384]{4,3,2,1,0:T(8,128)} %bitcast.51.refs_3_), custom_call_target="tpu_custom_call" | custom-call | bytes 4000000 | tf_op jit(solution)/shard_map/pallas_call | solution.py:61
  176.3 6.8 %fusion.59 = f32[1024,768]{1,0:T(8,128)} fusion(bf16[1024,1536]{1,0:T(8,128)(2,1)} %copy-done.48, bf16[1536,768]{1,0:T(8,128)(2,1)} %bitcast.141), kind=kOutput, calls=%fused_computation.156 | convolution fusion | flops 2415919104 | bytes 8650752 | tf_op jit(solution)/shard_map/dot_general | solution.py:946
  186.5 19.2 %shard_map.117 = (bf16[1024,384]{1,0:T(8,128)(2,1)}, bf16[1024,384]{1,0:T(8,128)(2,1)}, bf16[1024,384]{1,0:T(8,128)(2,1)}, bf16[1024,384]{1,0:T(8,128)(2,1)}, bf...) custom-call(s32[4]{0:T(128)} %fusion.50.plan_ref, bf16[1024,384]{1,0:T(8,128)(2,1)} %get-tuple-element.65.q_ref, ...), custom_call_target="tpu_custom_call" | custom-call | flops 40000000000 | bytes 10000000 | tf_op jit(solution)/shard_map/pallas_call | solution.py:670
  231.0 7.3 %shard_map.124 = (bf16[4,96,768]{2,1,0:T(8,128)(2,1)}, f32[4,96,768]{2,1,0:T(8,128)}, bf16[4,120,768]{2,1,0:T(8,128)(2,1)}, f32[4,120,768]{2,1,0:T(8,128)}) custom-call(s32[4]{0:T(128)} %pad_add_fusion.place_ref, f32[8,2,2,24,1536]{4,3,2,1,0:T(8,128)} %bitcast.97, f32[8,2,96,768]{3,2,1,0:T(8,128)} %bitcast.99, f32[4,2,2,24,384]{4,3,2,1,0:T(8,128)} %bitcast.123, ...), custom_call_target="tpu_custom_call" | custom-call | bytes 4000000 | tf_op jit(solution)/shard_map/pallas_call | solution.py:61
  238.3 3.5 collective-permute-start.37
  241.8 5.5 %collective-permute-done.24 = bf16[512,768]{1,0:T(8,128)(2,1)} collective-permute-done((bf16[512,768]{1,0:T(8,128)(2,1)}, bf16[512,768]{1,0:T(8,128)(2,1)}, u32[]{:S(2)}, u32[]{:S(2)}) %collective-permute-start.24) | collective-permute-done | bytes 786464 | tf_op jit(solution)/shard_map/ppermute | solution.py:958
  260.2 12.4 %collective-permute-done.25.refs_3_ = bf16[8,24,1280]{2,1,0:T(8,128)(2,1)} collective-permute-done((bf16[8,24,1280]{2,1,0:T(8,128)(2,1)}, bf16[8,24,1280]{2,1,0:T(8,128)(2,1)}, u32[]{:S(2)}, u32[]{:S(2)}) %collective-permute-start.25) | collective-permute-done | bytes 491552 | tf_op jit(solution)/shard_map/ppermute | solution.py:35
  272.6 3.7 shard_map.120
  277.6 7.4 %collective-permute-done.36.got_a = bf16[4,96,768]{2,1,0:T(8,128)(2,1)} collective-permute-done((bf16[4,96,768]{2,1,0:T(8,128)(2,1)}, bf16[4,96,768]{2,1,0:T(8,128)(2,1)}, u32[]{:S(2)}, u32[]{:S(2)}) %collective-permute-start.36) | collective-permute-done | bytes 589856 | tf_op jit(solution)/shard_map/ppermute | solution.py:35
  288.4 13.1 %collective-permute-start.38 = (bf16[216,768]{1,0:T(8,128)(2,1)}, bf16[216,768]{1,0:T(8,128)(2,1)S(1)}, u32[]{:S(2)}, u32[]{:S(2)}) collective-permute-start(bf16[216,768]{1,0:T(8,128)(2,1)} %get-tuple-element.105), channel_id=1, source_target_pairs={{0,8},{1,9},{2,10},{3,11},{4,12},{5,13},{6,14},{7,15},{8,0},{9,1},... | collective-permute-start | bytes 995336 | tf_op jit(solution)/shard_map/ppermute | solution.py:35
  305.8 4.8 %collective-permute-done.28.got_b = bf16[4,24,1280]{2,1,0:T(8,128)(2,1)} collective-permute-done((bf16[4,24,1280]{2,1,0:T(8,128)(2,1)}, bf16[4,24,1280]{2,1,0:T(8,128)(2,1)}, u32[]{:S(2)}, u32[]{:S(2)}) %collective-permute-start.28) | collective-permute-done | bytes 245792 | tf_op jit(solution)/shard_map/ppermute | solution.py:35
  316.5 13.0 %collective-permute-done.39.g2 = bf16[216,768]{1,0:T(8,128)(2,1)} collective-permute-done((bf16[216,768]{1,0:T(8,128)(2,1)}, bf16[216,768]{1,0:T(8,128)(2,1)}, u32[]{:S(2)}, u32[]{:S(2)}) %collective-permute-start.39) | collective-permute-done | bytes 331808 | tf_op jit(solution)/shard_map/ppermute | solution.py:35
  332.9 4.4 %collective-permute-done.30 = bf16[48,1280]{1,0:T(8,128)(2,1)} collective-permute-done((bf16[48,1280]{1,0:T(8,128)(2,1)}, bf16[48,1280]{1,0:T(8,128)(2,1)}, u32[]{:S(2)}, u32[]{:S(2)}) %collective-permute-start.30) | collective-permute-done | bytes 122912 | tf_op jit(solution)/shard_map/ppermute | solution.py:35
  356.9 3.9 %collective-permute-start.46 = (f32[8,128]{1,0:T(8,128)S(1)}, f32[8,128]{1,0:T(8,128)S(1)}, u32[]{:S(2)}, u32[]{:S(2)}) collective-permute-start(f32[8,128]{1,0:T(8,128)S(1)} %add.244), channel_id=1, source_target_pairs={{0,16},{1,17},{2,18},{3,19},{4,20},{5,21},{6,22},{7,23},{8,24},{9,... | collective-permute-start | bytes 12296 | tf_op jit(solution)/shard_map/ppermute | solution.py:35
  364.2 4.4 %shard_map.128 = (f32[1,221472]{1,0:T(1,128)}, f32[1,221472]{1,0:T(1,128)}, f32[1,221472]{1,0:T(1,128)}) custom-call(f32[8,128]{1,0:T(8,128)} %add.245.squares, f32[1,221472]{1,0:T(1,128)} %get-tuple-element.57.g_ref, f32[1,221472]{1,0:T(1,128)} %p_ref.1, f32[1,221472]{1,0:T(1,128)} %m_ref.1, f32[1,221472]{1,0:T(1,128)} %v_ref.1), custom_call_target="tpu_custom_call" | custom-call | bytes 6000000 | tf_op jit(solution)/shard_map/pallas_call | solution.py:426
  (282 shorter events, 146.2 us)
Async XLA Ops:
  0.7 13.1 %collective-permute-start = (s32[512]{0:T(512)}, s32[512]{0:T(512)S(1)}, u32[]{:S(2)}, u32[]{:S(2)}) collective-permute-start(s32[512]{0:T(512)} %param.9), channel_id=1, source_target_pairs={{0,2},{1,3},{2,0},{3,1},{4,6},{5,7},{6,4},{7,5},{8,10},{9,11},{10,... | collective-permute-start | bytes 6152 | tf_op jit(solution)/shard_map/ppermute | solution.py:35
  4.0 68.3 %collective-permute-start.1 = (bf16[512,768]{1,0:T(8,128)(2,1)}, bf16[512,768]{1,0:T(8,128)(2,1)}, u32[]{:S(2)}, u32[]{:S(2)}) collective-permute-start(bf16[512,768]{1,0:T(8,128)(2,1)} %param.7), channel_id=1, source_target_pairs={{0,2},{1,3},{2,0},{3,1},{4,6},{5,7},{6,4},{7,5},{8,10},{9,11},{10,... | collective-permute-start | bytes 2359304 | tf_op jit(solution)/shard_map/ppermute | solution.py:35
  39.4 12.8 %collective-permute-start.14 = (bf16[216,768]{1,0:T(8,128)(2,1)}, bf16[216,768]{1,0:T(8,128)(2,1)S(1)}, u32[]{:S(2)}, u32[]{:S(2)}) collective-permute-start(bf16[216,768]{1,0:T(8,128)(2,1)} %shard_map.115), channel_id=1, source_target_pairs={{0,24},{1,25},{2,26},{3,27},{4,28},{5,29},{6,30},{7,31},{8,16},{9,... | collective-permute-start | bytes 995336 | tf_op jit(solution)/shard_map/ppermute | solution.py:35
  41.9 27.3 %collective-permute-start.13 = (bf16[216,768]{1,0:T(8,128)(2,1)}, bf16[216,768]{1,0:T(8,128)(2,1)S(1)}, u32[]{:S(2)}, u32[]{:S(2)}) collective-permute-start(bf16[216,768]{1,0:T(8,128)(2,1)} %shard_map.115), channel_id=1, source_target_pairs={{0,16},{1,17},{2,18},{3,19},{4,20},{5,21},{6,22},{7,23},{8,24},{9,... | collective-permute-start | bytes 995336 | tf_op jit(solution)/shard_map/ppermute | solution.py:35
  41.9 27.8 %collective-permute-start.12 = (bf16[216,768]{1,0:T(8,128)(2,1)}, bf16[216,768]{1,0:T(8,128)(2,1)S(1)}, u32[]{:S(2)}, u32[]{:S(2)}) collective-permute-start(bf16[216,768]{1,0:T(8,128)(2,1)} %shard_map.115), channel_id=1, source_target_pairs={{0,8},{1,9},{2,10},{3,11},{4,12},{5,13},{6,14},{7,15},{8,0},{9,1},... | collective-permute-start | bytes 995336 | tf_op jit(solution)/shard_map/ppermute | solution.py:35
  45.6 33.3 %collective-permute-start.21 = (bf16[512,768]{1,0:T(8,128)(2,1)S(1)}, bf16[512,768]{1,0:T(8,128)(2,1)S(1)}, u32[]{:S(2)}, u32[]{:S(2)}) collective-permute-start(bf16[512,768]{1,0:T(8,128)(2,1)S(1)} %copy-done.8), channel_id=1, source_target_pairs={{0,2},{1,3},{2,0},{3,1},{4,6},{5,7},{6,4},{7,5},{8,10},{9,11},{10,... | collective-permute-start | bytes 2359304 | tf_op jit(solution)/shard_map/ppermute | solution.py:35
  52.2 23.9 %collective-permute-start.10 = (bf16[512,768]{1,0:T(8,128)(2,1)S(1)}, bf16[512,768]{1,0:T(8,128)(2,1)}, u32[]{:S(2)}, u32[]{:S(2)}) collective-permute-start(bf16[512,768]{1,0:T(8,128)(2,1)S(1)} %copy-done.11), channel_id=1, source_target_pairs={{0,1},{2,3},{4,5},{6,7},{8,9},{10,11},{12,13},{14,15},{16,17},{18,... | collective-permute-start | bytes 2359304 | tf_op jit(solution)/shard_map/ppermute | solution.py:801
  69.2 14.1 %collective-permute-start.9 = (bf16[2,4,1,24,1280]{4,3,1,2,0:T(8,128)(2,1)S(1)}, bf16[2,4,1,24,1280]{4,3,1,2,0:T(8,128)(2,1)S(1)}, u32[]{:S(2)}, u32[]{:S(2)}) collective-permute-start(bf16[2,4,1,24,1280]{4,3,1,2,0:T(8,128)(2,1)S(1)} %get-tuple-element.135), channel_id=1, source_target_pairs={{0,1},{1,0},{2,3},{3,2},{4,5},{5,4},{6,7},{7,6},{8,9},{9,8},{10,11... | collective-permute-start | bytes 1474568 | tf_op jit(solution)/shard_map/ppermute | solution.py:35
  69.7 14.1 %collective-permute-start.7 = (bf16[2,4,1,24,1280]{4,3,1,2,0:T(8,128)(2,1)S(1)}, bf16[2,4,1,24,1280]{4,3,1,2,0:T(8,128)(2,1)S(1)}, u32[]{:S(2)}, u32[]{:S(2)}) collective-permute-start(bf16[2,4,1,24,1280]{4,3,1,2,0:T(8,128)(2,1)S(1)} %get-tuple-element.141), channel_id=1, source_target_pairs={{0,4},{1,5},{2,6},{3,7},{4,0},{5,1},{6,2},{7,3},{8,12},{9,13},{10,... | collective-permute-start | bytes 1474568 | tf_op jit(solution)/shard_map/ppermute | solution.py:35
  72.3 28.5 %collective-permute-start.15 = (bf16[4,96,768]{2,1,0:T(8,128)(2,1)S(1)}, bf16[4,96,768]{2,1,0:T(8,128)(2,1)}, u32[]{:S(2)}, u32[]{:S(2)}) collective-permute-start(bf16[4,96,768]{2,1,0:T(8,128)(2,1)S(1)} %pad_maximum_fusion.5), channel_id=1, source_target_pairs={{0,1},{1,0},{2,3},{3,2},{4,5},{5,4},{6,7},{7,6},{8,9},{9,8},{10,11... | collective-permute-start | bytes 1769480 | tf_op jit(solution)/shard_map/ppermute | solution.py:35
  76.1 27.5 %collective-permute-start.17 = (bf16[4,120,768]{2,1,0:T(8,128)(2,1)}, bf16[4,120,768]{2,1,0:T(8,128)(2,1)}, u32[]{:S(2)}, u32[]{:S(2)}) collective-permute-start(bf16[4,120,768]{2,1,0:T(8,128)(2,1)} %pad_maximum_fusion.2), channel_id=1, source_target_pairs={{0,4},{1,5},{2,6},{3,7},{4,0},{5,1},{6,2},{7,3},{8,12},{9,13},{10,... | collective-permute-start | bytes 2211848 | tf_op jit(solution)/shard_map/ppermute | solution.py:35
  78.9 27.3 %collective-permute-start.11 = (bf16[512,768]{1,0:T(8,128)(2,1)}, bf16[512,768]{1,0:T(8,128)(2,1)}, u32[]{:S(2)}, u32[]{:S(2)}) collective-permute-start(bf16[512,768]{1,0:T(8,128)(2,1)} %collective-permute-done.10), channel_id=1, source_target_pairs={{0,2},{1,3},{2,0},{3,1},{4,6},{5,7},{6,4},{7,5},{8,10},{9,11},{10,... | collective-permute-start | bytes 2359304 | tf_op jit(solution)/shard_map/ppermute | solution.py:35
  103.1 31.6 %collective-permute-start.16 = (bf16[2,4,96,768]{3,2,1,0:T(8,128)(2,1)}, bf16[2,4,96,768]{3,2,1,0:T(8,128)(2,1)}, u32[]{:S(2)}, u32[]{:S(2)}) collective-permute-start(bf16[2,4,96,768]{3,2,1,0:T(8,128)(2,1)} %pad_maximum_fusion.1.a8), channel_id=1, source_target_pairs={{0,4},{1,5},{2,6},{3,7},{4,0},{5,1},{6,2},{7,3},{8,12},{9,13},{10,... | collective-permute-start | bytes 3538952 | tf_op jit(solution)/shard_map/ppermute | solution.py:35
  104.9 30.4 %collective-permute-start.18 = (bf16[2,4,120,768]{3,2,1,0:T(8,128)(2,1)S(1)}, bf16[2,4,120,768]{3,2,1,0:T(8,128)(2,1)}, u32[]{:S(2)}, u32[]{:S(2)}) collective-permute-start(bf16[2,4,120,768]{3,2,1,0:T(8,128)(2,1)S(1)} %pad_maximum_fusion.b8), channel_id=1, source_target_pairs={{0,1},{1,0},{2,3},{3,2},{4,5},{5,4},{6,7},{7,6},{8,9},{9,8},{10,11... | collective-permute-start | bytes 4423688 | tf_op jit(solution)/shard_map/ppermute | solution.py:35
  131.6 34.9 %collective-permute-start.33 = (f32[384,384]{1,0:T(8,128)}, f32[384,384]{1,0:T(8,128)}, u32[]{:S(2)}, u32[]{:S(2)}) collective-permute-start(f32[384,384]{1,0:T(8,128)} %fusion.26), channel_id=1, source_target_pairs={{0,2},{1,3},{2,0},{3,1},{4,6},{5,7},{6,4},{7,5},{8,10},{9,11},{10,... | collective-permute-start | bytes 1769480 | tf_op jit(solution)/shard_map/ppermute | solution.py:35
  161.5 21.6 %collective-permute-start.19 = (bf16[768,384]{1,0:T(8,128)(2,1)S(1)}, bf16[768,384]{1,0:T(8,128)(2,1)S(1)}, u32[]{:S(2)}, u32[]{:S(2)}) collective-permute-start(bf16[768,384]{1,0:T(8,128)(2,1)S(1)} %bitcast.120), channel_id=1, source_target_pairs={{0,2},{1,3},{2,0},{3,1},{4,6},{5,7},{6,4},{7,5},{8,10},{9,11},{10,... | collective-permute-start | bytes 1769480 | tf_op jit(solution)/shard_map/ppermute | solution.py:35
  172.4 58.5 %collective-permute-start.34 = (bf16[8,96,768]{2,1,0:T(8,128)(2,1)}, bf16[8,96,768]{2,1,0:T(8,128)(2,1)}, u32[]{:S(2)}, u32[]{:S(2)}) collective-permute-start(bf16[8,96,768]{2,1,0:T(8,128)(2,1)} %get-tuple-element.98), channel_id=1, source_target_pairs={{0,1},{1,0},{2,3},{3,2},{4,5},{5,4},{6,7},{7,6},{8,9},{9,8},{10,11... | collective-permute-start | bytes 3538952 | tf_op jit(solution)/shard_map/ppermute | solution.py:35
  175.6 55.4 %collective-permute-start.35 = (bf16[8,120,768]{2,1,0:T(8,128)(2,1)}, bf16[8,120,768]{2,1,0:T(8,128)(2,1)}, u32[]{:S(2)}, u32[]{:S(2)}) collective-permute-start(bf16[8,120,768]{2,1,0:T(8,128)(2,1)} %get-tuple-element.99), channel_id=1, source_target_pairs={{0,4},{1,5},{2,6},{3,7},{4,0},{5,1},{6,2},{7,3},{8,12},{9,13},{10,... | collective-permute-start | bytes 4423688 | tf_op jit(solution)/shard_map/ppermute | solution.py:35
  212.2 11.3 %collective-permute-start.23 = (f32[512,768]{1,0:T(8,128)S(1)}, f32[512,768]{1,0:T(8,128)S(1)}, u32[]{:S(2)}, u32[]{:S(2)}) collective-permute-start(f32[512,768]{1,0:T(8,128)S(1)} %slice.140), channel_id=1, source_target_pairs={{0,2},{1,3},{2,0},{3,1},{4,6},{5,7},{6,4},{7,5},{8,10},{9,11},{10,... | collective-permute-start | bytes 4718600 | tf_op jit(solution)/shard_map/ppermute | solution.py:35
  220.7 21.1 %collective-permute-start.22 = (f32[512,768]{1,0:T(8,128)}, f32[512,768]{1,0:T(8,128)}, u32[]{:S(2)}, u32[]{:S(2)}) collective-permute-start(f32[512,768]{1,0:T(8,128)} %slice.138), channel_id=1, source_target_pairs={{0,2},{1,3},{2,0},{3,1},{4,6},{5,7},{6,4},{7,5},{8,10},{9,11},{10,... | collective-permute-start | bytes 4718600 | tf_op jit(solution)/shard_map/ppermute | solution.py:35
  220.7 140.1 %collective-permute-start.20 = (f32[512,768]{1,0:T(8,128)}, f32[512,768]{1,0:T(8,128)}, u32[]{:S(2)}, u32[]{:S(2)}) collective-permute-start(f32[512,768]{1,0:T(8,128)} %slice.134), channel_id=1, source_target_pairs={{0,2},{1,3},{2,0},{3,1},{4,6},{5,7},{6,4},{7,5},{8,10},{9,11},{10,... | collective-permute-start | bytes 4718600 | tf_op jit(solution)/shard_map/ppermute | solution.py:35
  224.5 22.7 %collective-permute-start.24 = (bf16[512,768]{1,0:T(8,128)(2,1)}, bf16[512,768]{1,0:T(8,128)(2,1)}, u32[]{:S(2)}, u32[]{:S(2)}) collective-permute-start(bf16[512,768]{1,0:T(8,128)(2,1)} %fusion.13), channel_id=1, source_target_pairs={{1,0},{3,2},{5,4},{7,6},{9,8},{11,10},{13,12},{15,14},{17,16},{19,... | collective-permute-start | bytes 2359304 | tf_op jit(solution)/shard_map/ppermute | solution.py:958
  238.3 46.7 %collective-permute-start.37 = (bf16[4,120,768]{2,1,0:T(8,128)(2,1)}, bf16[4,120,768]{2,1,0:T(8,128)(2,1)}, u32[]{:S(2)}, u32[]{:S(2)}) collective-permute-start(bf16[4,120,768]{2,1,0:T(8,128)(2,1)} %get-tuple-element.103), channel_id=1, source_target_pairs={{0,1},{1,0},{2,3},{3,2},{4,5},{5,4},{6,7},{7,6},{8,9},{9,8},{10,11... | collective-permute-start | bytes 2211848 | tf_op jit(solution)/shard_map/ppermute | solution.py:35
  258.2 14.4 %collective-permute-start.25 = (bf16[8,24,1280]{2,1,0:T(8,128)(2,1)}, bf16[8,24,1280]{2,1,0:T(8,128)(2,1)}, u32[]{:S(2)}, u32[]{:S(2)}) collective-permute-start(bf16[8,24,1280]{2,1,0:T(8,128)(2,1)} %get-tuple-element.86), channel_id=1, source_target_pairs={{0,1},{1,0},{2,3},{3,2},{4,5},{5,4},{6,7},{7,6},{8,9},{9,8},{10,11... | collective-permute-start | bytes 1474568 | tf_op jit(solution)/shard_map/ppermute | solution.py:35
  258.2 14.4 %collective-permute-start.26 = (bf16[8,24,1280]{2,1,0:T(8,128)(2,1)}, bf16[8,24,1280]{2,1,0:T(8,128)(2,1)}, u32[]{:S(2)}, u32[]{:S(2)}) collective-permute-start(bf16[8,24,1280]{2,1,0:T(8,128)(2,1)} %get-tuple-element.87), channel_id=1, source_target_pairs={{0,4},{1,5},{2,6},{3,7},{4,0},{5,1},{6,2},{7,3},{8,12},{9,13},{10,... | collective-permute-start | bytes 1474568 | tf_op jit(solution)/shard_map/ppermute | solution.py:35
  259.5 25.5 %collective-permute-start.36 = (bf16[4,96,768]{2,1,0:T(8,128)(2,1)}, bf16[4,96,768]{2,1,0:T(8,128)(2,1)}, u32[]{:S(2)}, u32[]{:S(2)}) collective-permute-start(bf16[4,96,768]{2,1,0:T(8,128)(2,1)} %get-tuple-element.101), channel_id=1, source_target_pairs={{0,4},{1,5},{2,6},{3,7},{4,0},{5,1},{6,2},{7,3},{8,12},{9,13},{10,... | collective-permute-start | bytes 1769480 | tf_op jit(solution)/shard_map/ppermute | solution.py:35
  276.3 27.8 %collective-permute-start.27 = (bf16[4,24,1280]{2,1,0:T(8,128)(2,1)}, bf16[4,24,1280]{2,1,0:T(8,128)(2,1)}, u32[]{:S(2)}, u32[]{:S(2)}) collective-permute-start(bf16[4,24,1280]{2,1,0:T(8,128)(2,1)} %get-tuple-element.89), channel_id=1, source_target_pairs={{0,4},{1,5},{2,6},{3,7},{4,0},{5,1},{6,2},{7,3},{8,12},{9,13},{10,... | collective-permute-start | bytes 737288 | tf_op jit(solution)/shard_map/ppermute | solution.py:35
  288.4 25.4 %collective-permute-start.38 = (bf16[216,768]{1,0:T(8,128)(2,1)}, bf16[216,768]{1,0:T(8,128)(2,1)S(1)}, u32[]{:S(2)}, u32[]{:S(2)}) collective-permute-start(bf16[216,768]{1,0:T(8,128)(2,1)} %get-tuple-element.105), channel_id=1, source_target_pairs={{0,8},{1,9},{2,10},{3,11},{4,12},{5,13},{6,14},{7,15},{8,0},{9,1},... | collective-permute-start | bytes 995336 | tf_op jit(solution)/shard_map/ppermute | solution.py:35
  301.5 28.0 %collective-permute-start.39 = (bf16[216,768]{1,0:T(8,128)(2,1)}, bf16[216,768]{1,0:T(8,128)(2,1)}, u32[]{:S(2)}, u32[]{:S(2)}) collective-permute-start(bf16[216,768]{1,0:T(8,128)(2,1)} %get-tuple-element.106), channel_id=1, source_target_pairs={{0,16},{1,17},{2,18},{3,19},{4,20},{5,21},{6,22},{7,23},{8,24},{9,... | collective-permute-start | bytes 995336 | tf_op jit(solution)/shard_map/ppermute | solution.py:35
  302.6 27.9 %collective-permute-start.40 = (bf16[216,768]{1,0:T(8,128)(2,1)}, bf16[216,768]{1,0:T(8,128)(2,1)}, u32[]{:S(2)}, u32[]{:S(2)}) collective-permute-start(bf16[216,768]{1,0:T(8,128)(2,1)} %get-tuple-element.107), channel_id=1, source_target_pairs={{0,24},{1,25},{2,26},{3,27},{4,28},{5,29},{6,30},{7,31},{8,16},{9,... | collective-permute-start | bytes 995336 | tf_op jit(solution)/shard_map/ppermute | solution.py:35
  312.9 20.0 %collective-permute-start.29 = (bf16[48,1280]{1,0:T(8,128)(2,1)}, bf16[48,1280]{1,0:T(8,128)(2,1)}, u32[]{:S(2)}, u32[]{:S(2)}) collective-permute-start(bf16[48,1280]{1,0:T(8,128)(2,1)} %get-tuple-element.93), channel_id=1, source_target_pairs={{0,8},{1,9},{2,10},{3,11},{4,12},{5,13},{6,14},{7,15},{8,0},{9,1},... | collective-permute-start | bytes 368648 | tf_op jit(solution)/shard_map/ppermute | solution.py:35
  313.8 23.5 %collective-permute-start.30 = (bf16[48,1280]{1,0:T(8,128)(2,1)}, bf16[48,1280]{1,0:T(8,128)(2,1)}, u32[]{:S(2)}, u32[]{:S(2)}) collective-permute-start(bf16[48,1280]{1,0:T(8,128)(2,1)} %get-tuple-element.94), channel_id=1, source_target_pairs={{0,16},{1,17},{2,18},{3,19},{4,20},{5,21},{6,22},{7,23},{8,24},{9,... | collective-permute-start | bytes 368648 | tf_op jit(solution)/shard_map/ppermute | solution.py:35
  (65 other events, 486.1 us)
